TPU v7x, 128 devices: a whole 4x4x4 slice. The times are simulated.
128 devices in a mesh: slab: 32 (over z, x_lo, y), view: 4 (over x_hi, core).
Axes of the slice: x: 4 (x_hi: 2, x_lo: 2; x = x_hi * 2 + x_lo), y: 4, z: 4, core: 2. Of those that a mesh axis runs over, the one named last changes fastest.
Arguments:
- volume: float32 [128, 32, 128], P('slab', 'view'), may hold values from -6 to 6
- measured: float32 [4, 32, 4096], P('view', 'slab'), may hold values from -6 to 6
- dual_gain: float32 [4, 32, 4096], P('view', 'slab'), may hold values from 0.5 to 2
- pattern: int32 [4, 32, 64, 16], P(None, 'slab'), may hold values from 0 to 255
- angle: int32 [4, 32, 64], P(None, 'slab'), may hold values from 0 to 7
- response: bfloat16 [512, 1024], replicated, may hold values from -0.1875 to 0.1875
- w1: bfloat16 [9, 32, 6], replicated, may hold values from -0.875 to 0.875
- bias1: float32 [32], replicated, may hold values from -3 to 3
- w2: bfloat16 [9, 32, 96], replicated, may hold values from -0.21875 to 0.21875
- bias2: float32 [32], replicated, may hold values from -3 to 3
- w3: bfloat16 [9, 1, 96], replicated, may hold values from -0.21875 to 0.21875
- upstream: bfloat16 [128, 32, 128], P('slab', 'view'), may hold values from -6 to 6
Outputs:
- new_volume: float32 [128, 32, 128], P('slab', 'view')
- grad_volume: float32 [128, 32, 128], P('slab', 'view')
- grad_w1: float32 [9, 32, 6], replicated
- grad_bias1: float32 [32], replicated
- grad_w2: float32 [9, 32, 96], replicated
- grad_bias2: float32 [32], replicated
- grad_w3: float32 [9, 1, 96], replicated
Inputs may be any that keep to these rules, and one draw needn't show every extreme that they name: `pattern`: tile numbers within the band, numbered as in the first step.
All inputs are finite; a program needn't handle non-finite values.
Results may differ from a plain program's by a relative error of at most 0.025.
Values may be sent and summed in bfloat16 or wider, within the bound.
A program may use at most 192 MiB of HBM per device.

v0:
```python
import math

import jax
import jax.numpy as jnp
from jax import lax
from jax.sharding import PartitionSpec as P


def with_halo(block, sides, width):
    for axis, dim in sides:
        count = lax.axis_size(axis)
        forward = [(i, i + 1) for i in range(count - 1)]
        backward = [(target, source) for source, target in forward]
        low = lax.ppermute(
            lax.slice_in_dim(block, block.shape[dim] - width, None, axis=dim), axis, forward
        )
        high = lax.ppermute(lax.slice_in_dim(block, 0, width, axis=dim), axis, backward)
        block = jnp.concatenate([low, block, high], axis=dim)
    return block


def shift_x(source, offset):
    if offset == 0:
        return source
    zero_col = jnp.zeros(source.shape[:-1] + (1,), source.dtype)
    if offset == 1:
        return jnp.concatenate([source[..., 1:], zero_col], axis=-1)
    return jnp.concatenate([zero_col, source[..., :-1]], axis=-1)


def stacked_plane(padded, depth_off, row_off, slab_depth, slab_height):
    slice_cut = padded[:, depth_off : depth_off + slab_depth, row_off : row_off + slab_height, :]
    return jnp.concatenate([shift_x(slice_cut, col_off - 1) for col_off in range(3)], axis=0)


def conv_apply(padded, weight):
    slab_depth = padded.shape[1] - 2
    slab_height = padded.shape[2] - 2
    accumulated = jnp.zeros(
        (weight.shape[1], slab_depth, slab_height, padded.shape[3]), jnp.float32
    )
    for depth_off in range(3):
        for row_off in range(3):
            stacked = stacked_plane(padded, depth_off, row_off, slab_depth, slab_height)
            accumulated = accumulated + jnp.einsum(
                "ok,kzyx->ozyx",
                weight[depth_off * 3 + row_off],
                stacked,
                preferred_element_type=jnp.float32,
            )
    return accumulated


def conv_transpose(padded, weight):
    slab_depth = padded.shape[1] - 2
    slab_height = padded.shape[2] - 2
    channels = weight.shape[2] // 3
    accumulated = jnp.zeros((channels, slab_depth, slab_height, padded.shape[3]), jnp.float32)
    for depth_off in range(3):
        for row_off in range(3):
            slice_cut = padded[
                :,
                2 - depth_off : 2 - depth_off + slab_depth,
                2 - row_off : 2 - row_off + slab_height,
                :,
            ]
            partial_out = jnp.einsum(
                "ok,ozyx->kzyx",
                weight[depth_off * 3 + row_off],
                slice_cut,
                preferred_element_type=jnp.float32,
            )
            for col_off in range(3):
                accumulated = accumulated + shift_x(
                    partial_out[col_off * channels : (col_off + 1) * channels], 1 - col_off
                )
    return accumulated


def weight_grad(grad_out, padded):
    slab_depth = padded.shape[1] - 2
    slab_height = padded.shape[2] - 2
    pieces = []
    for depth_off in range(3):
        for row_off in range(3):
            stacked = stacked_plane(padded, depth_off, row_off, slab_depth, slab_height)
            pieces.append(
                jnp.einsum("ozyx,kzyx->ok", grad_out, stacked, preferred_element_type=jnp.float32)
            )
    return jnp.stack(pieces)


def silu_slope(values):
    sigma = jax.nn.sigmoid(values)
    return sigma * (1.0 + values * (1.0 - sigma))


def project_rows(tile_rows, tile_ids, angle_ids, response):
    row_count = tile_ids.shape[0]
    angles = response.shape[0] // 64
    picked = jnp.take(tile_rows, tile_ids.reshape(-1), axis=0).reshape(row_count, -1)
    spread = lax.dot_general(
        picked, response, (((1,), (1,)), ((), ())), preferred_element_type=jnp.float32
    )
    spread = spread.reshape(row_count, angles, 64)
    onehot = (angle_ids[:, None] == jnp.arange(angles, dtype=jnp.int32)[None, :]).astype(
        jnp.float32
    )
    return jnp.sum(spread * onehot[:, :, None], axis=1)


def backproject_rows(dual_rows, angle_ids, response):
    row_count = dual_rows.shape[0]
    angles = response.shape[0] // 64
    onehot = (angle_ids[:, None] == jnp.arange(angles, dtype=jnp.int32)[None, :]).astype(
        dual_rows.dtype
    )
    expanded = (onehot[:, :, None] * dual_rows[:, None, :]).reshape(row_count, angles * 64)
    contrib = jnp.dot(expanded, response, preferred_element_type=jnp.float32)
    return contrib.reshape(row_count * (response.shape[1] // 64), 64)


def local_tiles(field_in):
    slab_depth, slab_height, row_width = field_in.shape
    blocks = field_in.reshape(slab_depth // 4, 4, slab_height // 4, 4, row_width // 4, 4)
    return blocks.transpose(0, 2, 4, 1, 3, 5).reshape(-1, 64)


def local_field(tile_rows, slab_depth, slab_height, row_width):
    blocks = tile_rows.reshape(slab_depth // 4, slab_height // 4, row_width // 4, 4, 4, 4)
    return blocks.transpose(0, 3, 1, 4, 2, 5).reshape(slab_depth, slab_height, row_width)


def extend(field_in):
    return with_halo(field_in, (("slab", 1), ("view", 2)), 1)


def body(volume, measured, dual_gain, pattern, angle, response, w1, bias1, w2, bias2, w3, upstream):
    slab_depth, slab_height, row_width = volume.shape
    tile_count = slab_depth * slab_height * row_width // 64
    k_tiles = pattern.shape[3]
    member = lax.axis_index("view")
    pattern_band = pattern[:, 0]
    angle_band = angle[:, 0]

    def project(field_bf):
        tile_rows = local_tiles(field_bf)
        padded_rows = jnp.concatenate([tile_rows, jnp.zeros((1, 64), tile_rows.dtype)], axis=0)
        tile_index = pattern_band - member * tile_count
        inside = (tile_index >= 0) & (tile_index < tile_count)
        tile_index = jnp.where(inside, tile_index, tile_count)
        out_rows = project_rows(
            padded_rows, tile_index.reshape(-1, k_tiles), angle_band.reshape(-1), response
        )
        return (
            lax.psum_scatter(
                out_rows.reshape(1 * lax.axis_size("view"), -1).astype(jnp.bfloat16),
                "view",
                scatter_dimension=0,
                tiled=True,
            )
            .astype(jnp.float32)
            .reshape(1, 1, -1)
        )

    def backproject(dual_field):
        tile_index = pattern_band - member * tile_count
        inside = (tile_index >= 0) & (tile_index < tile_count)
        tile_index = jnp.where(inside, tile_index, tile_count)
        contrib = backproject_rows(
            lax.all_gather(dual_field.reshape(1, -1), "view", axis=0, tiled=True).reshape(-1, 64),
            angle_band.reshape(-1),
            response,
        )
        summed = jax.ops.segment_sum(contrib, tile_index.reshape(-1), num_segments=tile_count + 1)
        tile_sums_out = summed[:tile_count]
        return local_field(tile_sums_out, slab_depth, slab_height, row_width)

    projection = project(volume.astype(jnp.bfloat16))
    dual_field = (dual_gain * (projection - measured)).astype(jnp.bfloat16)
    back_field = backproject(dual_field)
    inputs = jnp.stack([volume, back_field]).astype(jnp.bfloat16)
    upward = upstream[None]
    inputs_pad = extend(inputs)
    first_pre = conv_apply(inputs_pad, w1) + bias1[:, None, None, None]
    hidden_one = jax.nn.silu(first_pre).astype(jnp.bfloat16)
    hidden_one_pad = extend(hidden_one)
    second_pre = conv_apply(hidden_one_pad, w2) + bias2[:, None, None, None]
    hidden_two = jax.nn.silu(second_pre).astype(jnp.bfloat16)
    hidden_two_pad = extend(hidden_two)
    new_volume = volume + conv_apply(hidden_two_pad, w3)[0]
    upward_pad = extend(upward)
    term_three = weight_grad(upward, hidden_two_pad)
    slope_two = (conv_transpose(upward_pad, w3) * silu_slope(second_pre)).astype(jnp.bfloat16)
    slope_two_pad = extend(slope_two)
    term_w2 = weight_grad(slope_two, hidden_one_pad)
    term_b2 = jnp.sum(slope_two.astype(jnp.float32), axis=(1, 2, 3))
    slope_one = (conv_transpose(slope_two_pad, w2) * silu_slope(first_pre)).astype(jnp.bfloat16)
    slope_one_pad = extend(slope_one)
    term_w1 = weight_grad(slope_one, inputs_pad)
    term_b1 = jnp.sum(slope_one.astype(jnp.float32), axis=(1, 2, 3))
    back_grad = conv_transpose(slope_one_pad, w1)
    grad_scale = 1.0 / math.sqrt(volume.size * lax.axis_size("slab") * lax.axis_size("view"))
    echo = (dual_gain * project(back_grad[1].astype(jnp.bfloat16))).astype(jnp.bfloat16)
    grad_volume = upstream.astype(jnp.float32) + back_grad[0] + backproject(echo)
    grad_three, grad_second, grad_bias_second, grad_first, grad_bias_first = lax.psum(
        (term_three, term_w2, term_b2, term_w1, term_b1), ("slab", "view")
    )
    return (
        new_volume,
        grad_volume,
        grad_first * grad_scale,
        grad_bias_first * grad_scale,
        grad_second * grad_scale,
        grad_bias_second * grad_scale,
        grad_three * grad_scale,
    )


def solution(mesh):
    placed = (
        P("slab", "view", None),
        P("view", "slab", None),
        P("view", "slab", None),
        P(None, "slab", None, None),
        P(None, "slab", None),
        P(),
        P(),
        P(),
        P(),
        P(),
        P(),
        P("slab", "view", None),
    )
    return jax.shard_map(
        body,
        mesh=mesh,
        in_specs=placed,
        out_specs=(P("slab", "view", None), P("slab", "view", None), P(), P(), P(), P(), P()),
        check_vma=False,
    )
```

profile of v0, /device:TPU:31, one launch (start us, length us, event | category | flops | bytes accessed | tf_op | source)
XLA Modules:
  0.0 524.0 jit_solution(18155029862642151852)
XLA Ops:
  8.0 3.5 collective-permute-start.12
  11.5 1.9 collective-permute-start.13
  16.5 1.3 reduce.7
  19.1 12.1 %gather_fusion = bf16[4096,64]{1,0:T(8,128)(2,1)S(1)} fusion(bf16[65,64]{1,0:T(8,128)(2,1)S(1)} %concatenate.613, s32[4096]{0:T(1024)S(1)} %fusion.280), kind=kCustom, calls=%fused_computation.clone | custom fusion | bytes 1064960 | tf_op jit(solution)/shard_map/jit(_take)/gather | solution.py:101
  31.2 2.1 broadcast_select_fusion.1
  34.9 13.6 %all-reduce.110 = bf16[4,4096]{1,0:T(4,128)(2,1)S(1)} all-reduce(bf16[4,4096]{1,0:T(4,128)(2,1)S(1)} %convert_element_type.73), channel_id=4, replica_groups=mesh['slab'=32,'view'=4] {'view'}, use_global_device_ids=true, to_apply=%region_1.3.clone | all-reduce | flops 16384 | bytes 65536
  49.7 7.6 %all-gather = bf16[4,1,4096]{2,1,0:T(2,128)(2,1)S(1)} all-gather(bf16[1,1,4096]{2,1,0:T(2,128)(2,1)S(1)} %fusion.261), channel_id=2, replica_groups=mesh['slab'=32,'view'=4] {'view'}, dimensions={0}, use_global_device_ids=true | all-gather | bytes 40960 | tf_op jit(solution)/shard_map/all_gather | solution.py:171
  58.1 1.9 reshape.389
  60.0 23.7 %scatter_custom_fusion = f32[65,64]{1,0:T(8,128)S(1)} fusion(s32[4096]{0:T(1024)S(1)} %bitcast.659, f32[4096,64]{1,0:T(8,128)} %reshape.389, f32[]{:T(128)} %constant.15.clone.1), kind=kCustom, calls=%fused_computation.421 | custom fusion | flops 262144 | bytes 17152 | tf_op jit(solution)/shard_map/scatter-add | solution.py:175
  84.7 6.3 %collective-permute-start = (bf16[2,1,8,128]{3,0,2,1:T(2,128)(2,1)S(1)}, bf16[2,1,8,128]{3,0,2,1:T(2,128)(2,1)S(1)}, u32[]{:S(2)}, u32[]{:S(2)}) collective-permute-start(bf16[2,1,8,128]{3,0,2,1:T(2,128)(2,1)S(1)} %get-tuple-element.152), channel_id=1, source_target_pairs={{0,4},{4,8},{8,12},{12,16},{16,20},{20,24},{24,28},{28,32},{32,36}... | collective-permute-start | bytes 12296 | tf_op jit(solution)/shard_map/ppermute | solution.py:14
  91.0 1.9 collective-permute-start.1
  93.6 2.2 collective-permute-start.14
  95.9 1.3 collective-permute-start.15
  97.2 3.3 collective-permute-done.15
  104.0 5.8 %collective-permute-start.3 = (bf16[2,6,1,128]{3,0,2,1:T(2,128)(2,1)S(1)}, bf16[2,6,1,128]{3,0,2,1:T(2,128)(2,1)S(1)}, u32[]{:S(2)}, u32[]{:S(2)}) collective-permute-start(bf16[2,6,1,128]{3,0,2,1:T(2,128)(2,1)S(1)} %get-tuple-element.148), channel_id=1, source_target_pairs={{1,0},{2,1},{3,2},{5,4},{6,5},{7,6},{9,8},{10,9},{11,10},{13,12},{... | collective-permute-start | bytes 9224 | tf_op jit(solution)/shard_map/ppermute | solution.py:17
  109.8 1.8 collective-permute-start.2
  116.2 1.2 multiply_convert_fusion.1
  117.4 5.8 %collective-permute-start.4 = (bf16[32,1,8,128]{3,0,2,1:T(8,128)(2,1)S(1)}, bf16[32,1,8,128]{3,0,2,1:T(8,128)(2,1)S(1)}, u32[]{:S(2)}, u32[]{:S(2)}) collective-permute-start(bf16[32,1,8,128]{3,0,2,1:T(8,128)(2,1)S(1)} %get-tuple-element.126), channel_id=1, source_target_pairs={{0,4},{4,8},{8,12},{12,16},{16,20},{20,24},{24,28},{28,32},{32,36}... | collective-permute-start | bytes 196616 | tf_op jit(solution)/shard_map/ppermute | solution.py:14
  123.2 1.9 collective-permute-start.5
  125.1 1.2 fusion.440
  126.3 4.9 collective-permute-done.5
  131.2 6.7 %collective-permute-start.7 = (bf16[32,6,1,128]{3,0,2,1:T(8,128)(2,1)S(1)}, bf16[32,6,1,128]{3,0,2,1:T(8,128)(2,1)S(1)}, u32[]{:S(2)}, u32[]{:S(2)}) collective-permute-start(bf16[32,6,1,128]{3,0,2,1:T(8,128)(2,1)S(1)} %get-tuple-element.98), channel_id=1, source_target_pairs={{1,0},{2,1},{3,2},{5,4},{6,5},{7,6},{9,8},{10,9},{11,10},{13,12},{... | collective-permute-start | bytes 147464 | tf_op jit(solution)/shard_map/ppermute | solution.py:17
  138.0 1.3 collective-permute-start.6
  139.8 1.3 collective-permute-done.6
  146.3 1.2 multiply_convert_fusion
  147.4 3.6 convert_reduce_fusion
  152.7 1.1 convolution_bitcast_fusion.8
  154.5 1.9 collective-permute-start.8
  156.4 3.5 collective-permute-start.9
  161.0 1.1 fusion.44
  162.1 1.1 fusion.43
  163.2 1.1 fusion.42
  164.3 1.1 fusion.41
  165.5 1.1 fusion.40
  167.7 1.1 fusion.38
  168.8 4.9 collective-permute-start.16
  173.7 1.9 collective-permute-start.17
  175.6 1.2 fusion.430
  176.8 135.1 %all-reduce.115.cloned.1.call-done = f32[9,32,96]{2,1,0:T(8,128)} async-done(((f32[9,32,96]{2,1,0:T(8,128)}), f32[9,32,96]{2,1,0:T(8,128)}) %all-reduce.115.cloned.1.call-update) | async-done | bytes 110608 | tf_op jit(solution)/shard_map/psum | solution.py:206
  311.9 1.6 broadcast_multiply_fusion.3
  314.2 1.3 collective-permute-start.10
  315.5 4.3 collective-permute-start.11
  321.7 1.2 fusion.179
  324.9 5.1 collective-permute-start.18
  330.1 1.3 collective-permute-start.19
  333.6 1.6 fusion.447
  335.2 1.5 fusion.445
  342.3 1.2 fusion.432
  343.9 1.1 fusion.426
  345.1 3.8 convert_reduce_fusion.1
  350.1 1.3 fusion.73
  359.7 66.1 %all-reduce.112 = (f32[9,32,6]{1,2,0:T(8,128)S(1)}, f32[32]{0:T(128)S(1)}, f32[32]{0:T(128)S(1)}, f32[9,1,96]{2,1,0:T(1,128)S(1)}) all-reduce(f32[9,32,6]{1,2,0:T(8,128)S(1)} %fusion.47, f32[32]{0:T(128)S(1)} %copy-done.136, f32[32]{0:T(128)S(1)} %copy-done.135, ...), channel_id=1, replica_groups=mesh['slab'=32,'view'=4] {'slab','view'}, use_global_device_ids=true, to_apply=%region_6.8 | all-reduce | flops 2656 | bytes 21248 | tf_op jit(solution)/shard_map/psum | solution.py:206
  427.6 2.4 collective-permute-start.20
  430.0 2.9 collective-permute-start.21
  434.1 4.0 collective-permute-done.21
  438.1 4.1 collective-permute-start.22
  442.2 1.3 collective-permute-start.23
  444.0 1.4 collective-permute-done.23
  448.5 12.1 %gather_fusion.1 = bf16[4096,64]{1,0:T(8,128)(2,1)S(1)} fusion(bf16[65,64]{1,0:T(8,128)(2,1)S(1)} %concatenate.779, s32[4096]{0:T(1024)S(1)} %fusion.280), kind=kCustom, calls=%fused_computation.1.clone | custom fusion | bytes 1064960 | tf_op jit(solution)/shard_map/jit(_take)/gather | solution.py:101
  460.7 2.1 broadcast_select_fusion
  464.3 16.8 %all-reduce.111 = bf16[4,4096]{1,0:T(4,128)(2,1)S(1)} all-reduce(bf16[4,4096]{1,0:T(4,128)(2,1)S(1)} %convert_element_type.82), channel_id=5, replica_groups=mesh['slab'=32,'view'=4] {'view'}, use_global_device_ids=true, to_apply=%region_4.6.clone | all-reduce | flops 16384 | bytes 65536
  481.7 7.4 %all-gather.1 = bf16[4,1,4096]{2,1,0:T(2,128)(2,1)S(1)} all-gather(bf16[1,1,4096]{2,1,0:T(2,128)(2,1)S(1)} %fusion.259), channel_id=3, replica_groups=mesh['slab'=32,'view'=4] {'view'}, dimensions={0}, use_global_device_ids=true | all-gather | bytes 40960 | tf_op jit(solution)/shard_map/all_gather | solution.py:171
  490.0 1.9 reshape.397
  491.9 23.7 %scatter_custom_fusion.1 = f32[65,64]{1,0:T(8,128)S(1)} fusion(s32[4096]{0:T(1024)} %bitcast.660, f32[4096,64]{1,0:T(8,128)} %reshape.397, f32[]{:T(128)} %constant.15.clone.1), kind=kCustom, calls=%fused_computation.419 | custom fusion | flops 262144 | bytes 17152 | tf_op jit(solution)/shard_map/scatter-add | solution.py:175
  (503 shorter events, 60.3 us)
Async XLA Ops:
  7.2 26.9 %copy-start = (bf16[512,1024]{1,0:T(8,128)(2,1)S(1)}, bf16[512,1024]{1,0:T(8,128)(2,1)}, u32[]{:S(2)}) copy-start(bf16[512,1024]{1,0:T(8,128)(2,1)} %param.19) | copy-start | bytes 3145732
  7.2 304.7 %all-reduce.115.cloned.1.call-start = ((), (), s32[]{:S(2)}) async-start(), calls=%async_computation | async-start | bytes 294912 | tf_op jit(solution)/shard_map/psum | solution.py:206
  8.0 85.6 %collective-permute-start.12 = (bf16[1,1,8,128]{3,2,1,0:T(8,128)(2,1)S(1)}, bf16[1,1,8,128]{3,2,1,0:T(8,128)(2,1)S(1)}, u32[]{:S(2)}, u32[]{:S(2)}) collective-permute-start(bf16[1,1,8,128]{3,2,1,0:T(8,128)(2,1)S(1)} %get-tuple-element.188), channel_id=1, source_target_pairs={{0,4},{4,8},{8,12},{12,16},{16,20},{20,24},{24,28},{28,32},{32,36}... | collective-permute-start | bytes 6152 | tf_op jit(solution)/shard_map/ppermute | solution.py:14
  11.5 82.1 %collective-permute-start.13 = (bf16[1,1,8,128]{3,2,1,0:T(8,128)(2,1)S(1)}, bf16[1,1,8,128]{3,2,1,0:T(8,128)(2,1)S(1)}, u32[]{:S(2)}, u32[]{:S(2)}) collective-permute-start(bf16[1,1,8,128]{3,2,1,0:T(8,128)(2,1)S(1)} %get-tuple-element.189), channel_id=1, source_target_pairs={{4,0},{8,4},{12,8},{16,12},{20,16},{24,20},{28,24},{32,28},{36,32}... | collective-permute-start | bytes 6152 | tf_op jit(solution)/shard_map/ppermute | solution.py:17
  18.0 16.1 %copy-start.133 = (f32[256,8]{0,1:T(8,128)}, f32[256,8]{0,1:T(8,128)S(1)}, u32[]{:S(2)}) copy-start(f32[256,8]{0,1:T(8,128)S(1)} %get-tuple-element.200) | copy-start | bytes 24580
  18.0 39.7 %copy-start.121 = (bf16[256,8]{0,1:T(8,128)(2,1)}, bf16[256,8]{0,1:T(8,128)(2,1)S(1)}, u32[]{:S(2)}) copy-start(bf16[256,8]{0,1:T(8,128)(2,1)S(1)} %get-tuple-element.199) | copy-start | bytes 12292
  18.0 42.0 %copy-start.131 = (s32[4096,1]{0,1:T(1,128)}, s32[4096,1]{0,1:T(1,128)S(1)}, u32[]{:S(2)}) copy-start(s32[4096,1]{0,1:T(1,128)S(1)} %and_select_fusion) | copy-start | bytes 49156
  34.1 14.4 %copy-start.139 = (u32[128]{0:T(128)S(1)}, u32[128]{0:T(128)}, u32[]{:S(2)}) copy-start(u32[128]{0:T(128)} %constant.266) | copy-start | bytes 1540
  34.1 14.9 %copy-start.114 = (f32[1,1,4096]{2,1,0:T(1,128)S(1)}, f32[1,1,4096]{2,1,0:T(1,128)}, u32[]{:S(2)}) copy-start(f32[1,1,4096]{2,1,0:T(1,128)} %param.16) | copy-start | bytes 49156
  34.1 14.9 %copy-start.132 = (f32[1,1,4096]{2,1,0:T(1,128)S(1)}, f32[1,1,4096]{2,1,0:T(1,128)}, u32[]{:S(2)}) copy-start(f32[1,1,4096]{2,1,0:T(1,128)} %param.15) | copy-start | bytes 49156
  58.1 34.8 %copy-start.64 = (bf16[4,8,128]{2,1,0:T(8,128)(2,1)S(1)}, bf16[4,8,128]{2,1,0:T(8,128)(2,1)}, u32[]{:S(2)}) copy-start(bf16[4,8,128]{2,1,0:T(8,128)(2,1)} %param.25) | copy-start | bytes 24580
  58.1 34.9 %copy-start.67 = (bf16[9,1,96]{2,0,1:T(8,128)(2,1)S(1)}, bf16[9,1,96]{2,0,1:T(8,128)(2,1)}, u32[]{:S(2)}) copy-start(bf16[9,1,96]{2,0,1:T(8,128)(2,1)} %param.24) | copy-start | bytes 5188
  84.7 19.3 %collective-permute-start = (bf16[2,1,8,128]{3,0,2,1:T(2,128)(2,1)S(1)}, bf16[2,1,8,128]{3,0,2,1:T(2,128)(2,1)S(1)}, u32[]{:S(2)}, u32[]{:S(2)}) collective-permute-start(bf16[2,1,8,128]{3,0,2,1:T(2,128)(2,1)S(1)} %get-tuple-element.152), channel_id=1, source_target_pairs={{0,4},{4,8},{8,12},{12,16},{16,20},{20,24},{24,28},{28,32},{32,36}... | collective-permute-start | bytes 12296 | tf_op jit(solution)/shard_map/ppermute | solution.py:14
  91.0 13.0 %collective-permute-start.1 = (bf16[2,1,8,128]{3,0,2,1:T(2,128)(2,1)S(1)}, bf16[2,1,8,128]{3,0,2,1:T(2,128)(2,1)S(1)}, u32[]{:S(2)}, u32[]{:S(2)}) collective-permute-start(bf16[2,1,8,128]{3,0,2,1:T(2,128)(2,1)S(1)} %get-tuple-element.153), channel_id=1, source_target_pairs={{4,0},{8,4},{12,8},{16,12},{20,16},{24,20},{28,24},{32,28},{36,32}... | collective-permute-start | bytes 12296 | tf_op jit(solution)/shard_map/ppermute | solution.py:17
  93.6 21.2 %copy-start.70 = (bf16[2,4,8,127]{3,0,2,1:T(2,128)(2,1)}, bf16[2,4,8,127]{3,0,2,1:T(2,128)(2,1)S(1)}, u32[]{:S(2)}) copy-start(bf16[2,4,8,127]{3,0,2,1:T(2,128)(2,1)S(1)} %slice_maximum_fusion) | copy-start | bytes 48772
  93.6 3.6 collective-permute-start.14
  95.9 4.6 collective-permute-start.15
  103.8 9.6 %copy-start.123 = (bf16[9,32,6]{1,2,0:T(8,128)(2,1)S(1)}, bf16[9,32,6]{1,2,0:T(8,128)(2,1)}, u32[]{:S(2)}) copy-start(bf16[9,32,6]{1,2,0:T(8,128)(2,1)} %param.20) | copy-start | bytes 10372
  104.0 7.8 %collective-permute-start.3 = (bf16[2,6,1,128]{3,0,2,1:T(2,128)(2,1)S(1)}, bf16[2,6,1,128]{3,0,2,1:T(2,128)(2,1)S(1)}, u32[]{:S(2)}, u32[]{:S(2)}) collective-permute-start(bf16[2,6,1,128]{3,0,2,1:T(2,128)(2,1)S(1)} %get-tuple-element.148), channel_id=1, source_target_pairs={{1,0},{2,1},{3,2},{5,4},{6,5},{7,6},{9,8},{10,9},{11,10},{13,12},{... | collective-permute-start | bytes 9224 | tf_op jit(solution)/shard_map/ppermute | solution.py:17
  109.8 3.1 collective-permute-start.2
  111.8 4.1 copy-start.100
  111.8 4.1 copy-start.102
  111.8 4.1 copy-start.96
  117.4 8.9 %collective-permute-start.4 = (bf16[32,1,8,128]{3,0,2,1:T(8,128)(2,1)S(1)}, bf16[32,1,8,128]{3,0,2,1:T(8,128)(2,1)S(1)}, u32[]{:S(2)}, u32[]{:S(2)}) collective-permute-start(bf16[32,1,8,128]{3,0,2,1:T(8,128)(2,1)S(1)} %get-tuple-element.126), channel_id=1, source_target_pairs={{0,4},{4,8},{8,12},{12,16},{16,20},{20,24},{24,28},{28,32},{32,36}... | collective-permute-start | bytes 196616 | tf_op jit(solution)/shard_map/ppermute | solution.py:14
  123.2 8.0 %collective-permute-start.5 = (bf16[32,1,8,128]{3,0,2,1:T(8,128)(2,1)S(1)}, bf16[32,1,8,128]{3,0,2,1:T(8,128)(2,1)S(1)}, u32[]{:S(2)}, u32[]{:S(2)}) collective-permute-start(bf16[32,1,8,128]{3,0,2,1:T(8,128)(2,1)S(1)} %get-tuple-element.127), channel_id=1, source_target_pairs={{4,0},{8,4},{12,8},{16,12},{20,16},{24,20},{28,24},{32,28},{36,32}... | collective-permute-start | bytes 196616 | tf_op jit(solution)/shard_map/ppermute | solution.py:17
  131.2 8.5 %collective-permute-start.7 = (bf16[32,6,1,128]{3,0,2,1:T(8,128)(2,1)S(1)}, bf16[32,6,1,128]{3,0,2,1:T(8,128)(2,1)S(1)}, u32[]{:S(2)}, u32[]{:S(2)}) collective-permute-start(bf16[32,6,1,128]{3,0,2,1:T(8,128)(2,1)S(1)} %get-tuple-element.98), channel_id=1, source_target_pairs={{1,0},{2,1},{3,2},{5,4},{6,5},{7,6},{9,8},{10,9},{11,10},{13,12},{... | collective-permute-start | bytes 147464 | tf_op jit(solution)/shard_map/ppermute | solution.py:17
  138.0 3.1 collective-permute-start.6
  139.4 4.1 copy-start.24
  139.4 5.1 copy-start.20
  139.4 5.1 copy-start.22
  139.4 6.2 %copy-start.18 = (bf16[32,4,8,127]{3,0,2,1:T(8,128)(2,1)}, bf16[32,4,8,127]{3,0,2,1:T(8,128)(2,1)S(1)}, u32[]{:S(2)}) copy-start(bf16[32,4,8,127]{3,0,2,1:T(8,128)(2,1)S(1)} %get-tuple-element.122) | copy-start | bytes 780292
  139.7 5.9 %copy-start.46 = (bf16[32,4,8,128]{3,0,2,1:T(8,128)(2,1)}, bf16[32,4,8,128]{3,0,2,1:T(8,128)(2,1)S(1)}, u32[]{:S(2)}) copy-start(bf16[32,4,8,128]{3,0,2,1:T(8,128)(2,1)S(1)} %get-tuple-element.104) | copy-start | bytes 786436
  139.7 5.9 %copy-start.48 = (bf16[32,4,8,128]{3,0,2,1:T(8,128)(2,1)}, bf16[32,4,8,128]{3,0,2,1:T(8,128)(2,1)S(1)}, u32[]{:S(2)}) copy-start(bf16[32,4,8,128]{3,0,2,1:T(8,128)(2,1)S(1)} %get-tuple-element.105) | copy-start | bytes 786436
  141.3 4.0 copy-start.50
  141.8 4.2 copy-start.56
  151.0 8.9 %copy-start.25 = (bf16[32,4,8,127]{3,0,2,1:T(8,128)(2,1)S(1)}, bf16[32,4,8,127]{3,0,2,1:T(8,128)(2,1)}, u32[]{:S(2)}) copy-start(bf16[32,4,8,127]{3,0,2,1:T(8,128)(2,1)} %copy-done.24) | copy-start | bytes 780292
  151.0 8.9 %copy-start.53 = (bf16[32,4,8,128]{3,0,2,1:T(8,128)(2,1)S(1)}, bf16[32,4,8,128]{3,0,2,1:T(8,128)(2,1)}, u32[]{:S(2)}) copy-start(bf16[32,4,8,128]{3,0,2,1:T(8,128)(2,1)} %copy-done.52) | copy-start | bytes 786436
  151.0 8.9 %copy-start.55 = (bf16[32,4,8,128]{3,0,2,1:T(8,128)(2,1)S(1)}, bf16[32,4,8,128]{3,0,2,1:T(8,128)(2,1)}, u32[]{:S(2)}) copy-start(bf16[32,4,8,128]{3,0,2,1:T(8,128)(2,1)} %copy-done.54) | copy-start | bytes 786436
  154.5 159.0 %collective-permute-start.8 = (bf16[32,1,8,128]{3,0,2,1:T(8,128)(2,1)}, bf16[32,1,8,128]{3,0,2,1:T(8,128)(2,1)S(1)}, u32[]{:S(2)}, u32[]{:S(2)}) collective-permute-start(bf16[32,1,8,128]{3,0,2,1:T(8,128)(2,1)} %get-tuple-element.118), channel_id=1, source_target_pairs={{0,4},{4,8},{8,12},{12,16},{16,20},{20,24},{24,28},{28,32},{32,36}... | collective-permute-start | bytes 196616 | tf_op jit(solution)/shard_map/ppermute | solution.py:14
  156.4 4.6 copy-start.43
  156.4 4.6 copy-start.45
  156.4 4.6 copy-start.63
  156.4 157.1 %collective-permute-start.9 = (bf16[32,1,8,128]{3,0,2,1:T(8,128)(2,1)}, bf16[32,1,8,128]{3,0,2,1:T(8,128)(2,1)}, u32[]{:S(2)}, u32[]{:S(2)}) collective-permute-start(bf16[32,1,8,128]{3,0,2,1:T(8,128)(2,1)} %get-tuple-element.119), channel_id=1, source_target_pairs={{4,0},{8,4},{12,8},{16,12},{20,16},{24,20},{28,24},{32,28},{36,32}... | collective-permute-start | bytes 196616 | tf_op jit(solution)/shard_map/ppermute | solution.py:17
  167.7 6.0 %copy-start.116 = (bf16[32,1,8,128]{3,0,2,1:T(8,128)(2,1)S(1)}, bf16[32,1,8,128]{3,0,2,1:T(8,128)(2,1)}, u32[]{:S(2)}) copy-start(bf16[32,1,8,128]{3,0,2,1:T(8,128)(2,1)} %get-tuple-element.111) | copy-start | bytes 196612
  168.8 156.1 %collective-permute-start.16 = (bf16[32,1,8,128]{3,0,2,1:T(8,128)(2,1)S(1)}, bf16[32,1,8,128]{3,0,2,1:T(8,128)(2,1)S(1)}, u32[]{:S(2)}, u32[]{:S(2)}) collective-permute-start(bf16[32,1,8,128]{3,0,2,1:T(8,128)(2,1)S(1)} %copy-done.117), channel_id=1, source_target_pairs={{0,4},{4,8},{8,12},{12,16},{16,20},{20,24},{24,28},{28,32},{32,36}... | collective-permute-start | bytes 196616 | tf_op jit(solution)/shard_map/ppermute | solution.py:14
  173.7 151.2 %collective-permute-start.17 = (bf16[32,1,8,128]{3,0,2,1:T(8,128)(2,1)S(1)}, bf16[32,1,8,128]{3,0,2,1:T(8,128)(2,1)S(1)}, u32[]{:S(2)}, u32[]{:S(2)}) collective-permute-start(bf16[32,1,8,128]{3,0,2,1:T(8,128)(2,1)S(1)} %copy-done.116), channel_id=1, source_target_pairs={{4,0},{8,4},{12,8},{16,12},{20,16},{24,20},{28,24},{32,28},{36,32}... | collective-permute-start | bytes 196616 | tf_op jit(solution)/shard_map/ppermute | solution.py:17
  314.2 18.4 %collective-permute-start.10 = (bf16[32,6,1,128]{3,0,2,1:T(8,128)(2,1)S(1)}, bf16[32,6,1,128]{3,0,2,1:T(8,128)(2,1)S(1)}, u32[]{:S(2)}, u32[]{:S(2)}) collective-permute-start(bf16[32,6,1,128]{3,0,2,1:T(8,128)(2,1)S(1)} %get-tuple-element.94), channel_id=1, source_target_pairs={{0,1},{1,2},{2,3},{4,5},{5,6},{6,7},{8,9},{9,10},{10,11},{12,13},{... | collective-permute-start | bytes 147464 | tf_op jit(solution)/shard_map/ppermute | solution.py:14
  315.5 17.1 %collective-permute-start.11 = (bf16[32,6,1,128]{3,0,2,1:T(8,128)(2,1)S(1)}, bf16[32,6,1,128]{3,0,2,1:T(8,128)(2,1)S(1)}, u32[]{:S(2)}, u32[]{:S(2)}) collective-permute-start(bf16[32,6,1,128]{3,0,2,1:T(8,128)(2,1)S(1)} %get-tuple-element.95), channel_id=1, source_target_pairs={{1,0},{2,1},{3,2},{5,4},{6,5},{7,6},{9,8},{10,9},{11,10},{13,12},{... | collective-permute-start | bytes 147464 | tf_op jit(solution)/shard_map/ppermute | solution.py:17
  323.9 7.5 %copy-start.69 = (bf16[9,32,96]{2,1,0:T(8,128)(2,1)S(1)}, bf16[9,32,96]{2,1,0:T(8,128)(2,1)}, u32[]{:S(2)}) copy-start(bf16[9,32,96]{2,1,0:T(8,128)(2,1)} %param.22) | copy-start | bytes 165892
  324.9 15.6 %collective-permute-start.18 = (bf16[32,6,1,128]{3,0,2,1:T(8,128)(2,1)S(1)}, bf16[32,6,1,128]{3,0,2,1:T(8,128)(2,1)S(1)}, u32[]{:S(2)}, u32[]{:S(2)}) collective-permute-start(bf16[32,6,1,128]{3,0,2,1:T(8,128)(2,1)S(1)} %get-tuple-element.90), channel_id=1, source_target_pairs={{1,0},{2,1},{3,2},{5,4},{6,5},{7,6},{9,8},{10,9},{11,10},{13,12},{... | collective-permute-start | bytes 147464 | tf_op jit(solution)/shard_map/ppermute | solution.py:17
  330.1 7.6 %collective-permute-start.19 = (bf16[32,6,1,128]{3,0,2,1:T(8,128)(2,1)S(1)}, bf16[32,6,1,128]{3,0,2,1:T(8,128)(2,1)S(1)}, u32[]{:S(2)}, u32[]{:S(2)}) collective-permute-start(bf16[32,6,1,128]{3,0,2,1:T(8,128)(2,1)S(1)} %get-tuple-element.91), channel_id=1, source_target_pairs={{0,1},{1,2},{2,3},{4,5},{5,6},{6,7},{8,9},{9,10},{10,11},{12,13},{... | collective-permute-start | bytes 147464 | tf_op jit(solution)/shard_map/ppermute | solution.py:14
  358.6 74.3 %copy-start.65 = (f32[4,8,128]{2,1,0:T(8,128)S(1)}, f32[4,8,128]{2,1,0:T(8,128)}, u32[]{:S(2)}) copy-start(f32[4,8,128]{2,1,0:T(8,128)} %param.14) | copy-start | bytes 49156
  358.6 74.3 %copy-start.118 = (f32[1,4,8,128]{3,0,2,1:T(1,128)S(1)}, f32[1,4,8,128]{3,0,2,1:T(1,128)}, u32[]{:S(2)}) copy-start(f32[1,4,8,128]{3,0,2,1:T(1,128)} %fusion.375) | copy-start | bytes 49156
  358.6 74.3 %copy-start.119 = (f32[1,4,8,128]{3,0,2,1:T(1,128)S(1)}, f32[1,4,8,128]{3,0,2,1:T(1,128)}, u32[]{:S(2)}) copy-start(f32[1,4,8,128]{3,0,2,1:T(1,128)} %fusion.381) | copy-start | bytes 49156
  358.6 74.3 %copy-start.120 = (f32[1,4,8,128]{3,0,2,1:T(1,128)S(1)}, f32[1,4,8,128]{3,0,2,1:T(1,128)}, u32[]{:S(2)}) copy-start(f32[1,4,8,128]{3,0,2,1:T(1,128)} %fusion.369) | copy-start | bytes 49156
  358.9 84.6 %copy-start.124 = (bf16[9,32,6]{1,2,0:T(8,128)(2,1)S(1)}, bf16[9,32,6]{1,2,0:T(8,128)(2,1)}, u32[]{:S(2)}) copy-start(bf16[9,32,6]{1,2,0:T(8,128)(2,1)} %param.20) | copy-start | bytes 10372
  427.6 6.5 %collective-permute-start.20 = (bf16[32,1,8,128]{3,0,2,1:T(8,128)(2,1)S(1)}, bf16[32,1,8,128]{3,0,2,1:T(8,128)(2,1)S(1)}, u32[]{:S(2)}, u32[]{:S(2)}) collective-permute-start(bf16[32,1,8,128]{3,0,2,1:T(8,128)(2,1)S(1)} %get-tuple-element.108), channel_id=1, source_target_pairs={{0,4},{4,8},{8,12},{12,16},{16,20},{20,24},{24,28},{28,32},{32,36}... | collective-permute-start | bytes 196616 | tf_op jit(solution)/shard_map/ppermute | solution.py:14
  430.0 8.0 %collective-permute-start.21 = (bf16[32,1,8,128]{3,0,2,1:T(8,128)(2,1)S(1)}, bf16[32,1,8,128]{3,0,2,1:T(8,128)(2,1)S(1)}, u32[]{:S(2)}, u32[]{:S(2)}) collective-permute-start(bf16[32,1,8,128]{3,0,2,1:T(8,128)(2,1)S(1)} %get-tuple-element.109), channel_id=1, source_target_pairs={{4,0},{8,4},{12,8},{16,12},{20,16},{24,20},{28,24},{32,28},{36,32}... | collective-permute-start | bytes 196616 | tf_op jit(solution)/shard_map/ppermute | solution.py:17
  438.1 8.1 %collective-permute-start.22 = (bf16[32,6,1,128]{3,0,2,1:T(8,128)(2,1)S(1)}, bf16[32,6,1,128]{3,0,2,1:T(8,128)(2,1)S(1)}, u32[]{:S(2)}, u32[]{:S(2)}) collective-permute-start(bf16[32,6,1,128]{3,0,2,1:T(8,128)(2,1)S(1)} %get-tuple-element.88), channel_id=1, source_target_pairs={{1,0},{2,1},{3,2},{5,4},{6,5},{7,6},{9,8},{10,9},{11,10},{13,12},{... | collective-permute-start | bytes 147464 | tf_op jit(solution)/shard_map/ppermute | solution.py:17
  442.2 3.2 collective-permute-start.23
  447.4 13.3 %copy-start.66 = (f32[2,4,8,128]{3,0,2,1:T(2,128)}, f32[2,4,8,128]{3,0,2,1:T(2,128)S(1)}, u32[]{:S(2)}) copy-start(f32[2,4,8,128]{3,0,2,1:T(2,128)S(1)} %fusion.234) | copy-start | bytes 98308
  463.5 17.5 %copy-start.115 = (f32[1,1,4096]{2,1,0:T(1,128)S(1)}, f32[1,1,4096]{2,1,0:T(1,128)}, u32[]{:S(2)}) copy-start(f32[1,1,4096]{2,1,0:T(1,128)} %param.16) | copy-start | bytes 49156
  463.6 25.9 %copy-start.122 = (bf16[256,8]{0,1:T(8,128)(2,1)S(1)}, bf16[256,8]{0,1:T(8,128)(2,1)}, u32[]{:S(2)}) copy-start(bf16[256,8]{0,1:T(8,128)(2,1)} %copy-done.121) | copy-start | bytes 12292
  490.0 26.4 %slice-start = ((f32[2,4,8,128]{3,0,2,1:T(2,128)}), f32[1,4,8,128]{3,0,2,1:T(1,128)S(1)}, s32[]{:S(2)}) async-start(f32[2,4,8,128]{3,0,2,1:T(2,128)} %copy-done.66), calls=%async_computation.1 | async-start | bytes 32768 | tf_op jit(solution)/shard_map/slice | solution.py:205
  (102 other events, 172.0 us)
Sparse Core Ops, SparseCore 0:
  168.9 142.9 all-reduce.114
where the time goes:
time: 533 us; the launch traced here: 524 us
  waiting for transfers between devices  151 us (28%)
  blocking collectives  111 us (21%)
  other arithmetic  79.4 us (15%)
  starting transfers between devices  75.3 us (14%)
  local copies, waits for them, and re-layouts  56.1 us (11%)
  matrix products  33.9 us (6%)
  between operations  16.9 us (3%)
    psum x1, waiting for transfers between devices, body(): lax.psum((term_three, term_w2, term_b2, term_w1, term_b1), ('slab', 'view'))  135 us
    psum x1, blocking collectives, body(): lax.psum((term_three, term_w2, term_b2, term_w1, term_b1), ('slab', 'view'))  66.1 us
    scatter-add x2, other arithmetic, backproject(): jax.ops.segment_sum(contrib, tile_index.reshape(-1), num_segments=tile_co...  47.4 us
    ppermute x12, starting transfers between devices, with_halo(): lax.ppermute(lax.slice_in_dim(block, 0, width, axis=dim), axis, backward)  42.3 us
    ppermute x12, starting transfers between devices, with_halo(): lax.ppermute(lax.slice_in_dim(block, block.shape[dim] - width, None, axis...  33 us
    unnamed x2, blocking collectives  30.4 us
    gather x2, local copies, waits for them, and re-layouts, project_rows(): jnp.take(tile_rows, tile_ids.reshape(-1), axis=0).reshape(row_count, -1)  24.3 us
    all_gather x2, blocking collectives, backproject(): lax.all_gather(dual_field.reshape(1, -1), 'view', axis=0, tiled=True)  14.9 us
  transfers between devices with their start and end apart: 25, of which 7 were waited for; matrix products, arithmetic and copies ran while one was open for 16% of the time, Pallas kernels for 0%

commit v1 on v0

v1 whole, which is shorter than its diff:
```python
import functools
import math

import jax
import jax.numpy as jnp
import ml_dtypes
import numpy as np
from jax import lax
from jax.experimental import pallas as pl
from jax.experimental.pallas import tpu as pltpu
from jax.sharding import PartitionSpec as P

F32 = jnp.float32
BF16 = jnp.bfloat16
MESH = pl.DeviceIdType.MESH
VIEWS = 4
RING = 8
LAYERS = 4
SLABS = RING * LAYERS
PIECE = 5
VMEM_BYTES = 50 * 1024 * 1024


def mm(a, b):
    return lax.dot_general(a, b, (((1,), (0,)), ((), ())), preferred_element_type=F32)


def mmt(a, b):
    return lax.dot_general(a, b, (((1,), (1,)), ((), ())), preferred_element_type=F32)


def iota(shape, dim):
    return lax.broadcasted_iota(jnp.int32, shape, dim)


def one(cond):
    return jnp.where(cond, 1.0, 0.0).astype(BF16)


def host_bf16(cond):
    return np.asarray(cond, np.float32).astype(ml_dtypes.bfloat16)


def tile_constants():
    row, col = np.arange(128)[:, None], np.arange(128)[None, :]
    pick_x = host_bf16(col == 4 * (row % 32) + row // 32)
    r, c = np.arange(512)[:, None], np.arange(1024)[None, :]
    xi, quarter, z, y8 = r // 128, r // 32 % 4, r // 8 % 4, r % 8
    yt, j = c // 128, c % 64
    place = host_bf16(
        (2 * quarter + y8 // 4 == yt) & (z == j // 16) & (y8 % 4 == j // 4 % 4) & (xi == j % 4)
    )
    r, c = np.arange(64)[:, None], np.arange(128)[None, :]
    pick_j = host_bf16((c < 64) & (c % 4 == r // 16) & (c // 4 == r % 16))
    r, c = np.arange(512)[:, None], np.arange(512)[None, :]
    spread_x = host_bf16((r // 32 % 4 == c // 128) & (c % 128 == 4 * (r % 32) + r // 128))
    return pick_x, place, pick_j, spread_x


def weight_constants():
    lane = np.arange(384)
    band1 = np.zeros((9, 6, 384), np.float32)
    for a in range(3):
        for b in range(3):
            for e in range(3):
                for c in range(2):
                    band1[3 * a + b, 2 * e + c, ((a * 2 + c) * 3 + e) * 16 + b] = 1.0
    band3 = np.zeros((3, 9, 256), np.float32)
    for a in range(3):
        for b in range(3):
            for e in range(3):
                band3[e, 3 * (2 - a) + (2 - b), (a * 3 + e) * 16 + b] = 1.0
    rep3 = np.zeros((3, 96, 384), np.float32)
    for e in range(3):
        rep3[e, 32 * e + lane % 32, lane] = 1.0
    fold1 = np.zeros((384, 1152), np.float32)
    for a in range(3):
        for b in range(3):
            for e in range(3):
                for c in range(2):
                    fold1[
                        ((a * 2 + c) * 3 + e) * 16 + 3 + b, 128 * (3 * a + b) + 97 + 2 * e + c
                    ] = 1.0
    fold1[288, 103] = 1.0
    fold3 = np.zeros((3, 384, 128), np.float32)
    for e in range(3):
        live = lane[lane < 320]
        fold3[e, live, 32 * e + live % 32] = 1.0
    return tuple(host_bf16(x) for x in (band1, band3, rep3, fold1, fold3))


def own_order():
    return one(iota((64, 64), 1) == 2 * (iota((64, 64), 0) % 32) + iota((64, 64), 0) // 32)


def view_choice(pattern_ref, angle_ref, member):
    order = own_order()
    ids = mm(order, pattern_ref[member].astype(F32).astype(BF16)).astype(jnp.int32)
    lanes = iota((64, 256), 1)
    choice = jnp.concatenate([one(lanes == ids[:, k : k + 1]) for k in range(16)], axis=0)
    angles = mmt(order, angle_ref[...].astype(F32).astype(BF16)).astype(jnp.int32)
    mine = jnp.sum(jnp.where(iota((64, 4), 1) == member, angles, 0), axis=1, keepdims=True)
    return choice, mine


def band_choice(pattern_ref, angle_ref, first, count):
    order = own_order()
    rows = jnp.concatenate(
        [mm(order, pattern_ref[g].astype(F32).astype(BF16)) for g in range(VIEWS)], axis=0
    )
    eye = one(iota((16, 16), 0) == iota((16, 16), 1))
    ids = mmt(eye, rows.astype(BF16)).astype(jnp.int32)
    tile = iota((count, 256), 0) + first
    even = jnp.concatenate([one(tile == ids[k : k + 1, :]) for k in range(0, 16, 2)], axis=1)
    odd = jnp.concatenate([one(tile == ids[k : k + 1, :]) for k in range(1, 16, 2)], axis=1)
    angles = mmt(order, angle_ref[...].astype(F32).astype(BF16)).astype(jnp.int32)
    column = jnp.concatenate([angles[:, g : g + 1] for g in range(VIEWS)], axis=0)
    return jnp.concatenate([even, odd], axis=0), column


def project(field_rows, choice, angles, response_ref, pick_x_ref, place_ref):
    by_x = mmt(pick_x_ref[...], field_rows).astype(BF16)
    wide = jnp.concatenate([by_x[32 * i : 32 * i + 32] for i in range(4)], axis=1)
    spread = mm(wide, place_ref[...]).astype(BF16)
    tiles = jnp.concatenate([spread[:, 128 * i : 128 * i + 128] for i in range(8)], axis=0)
    picked = mm(choice, tiles)
    low = iota((64, 128), 1) < 64
    pairs = [
        jnp.where(low, picked[128 * p : 128 * p + 64], picked[128 * p + 64 : 128 * p + 128])
        for p in range(8)
    ]
    lines = mmt(jnp.concatenate(pairs, axis=1).astype(BF16), response_ref[...])
    half = iota((64, 128), 1) // 64
    total = jnp.zeros((64, 128), F32)
    for p in range(4):
        total = total + jnp.where(angles == 2 * p + half, lines[:, 128 * p : 128 * p + 128], 0.0)
    total = total + pltpu.roll(total, 64, 1)
    return jnp.where(low[:32], total[:32], total[32:])


def backproject(rows_ref, chosen, angles, response_ref, pick_j_ref, spread_x_ref, count):
    low = iota((32, 128), 1) < 64
    parts = []
    for g in range(VIEWS):
        rows = rows_ref[g].astype(F32)
        turned = pltpu.roll(rows, 64, 1)
        parts.append(jnp.where(low, rows, turned))
        parts.append(jnp.where(low, turned, rows))
    doubled = jnp.concatenate(parts, axis=0)
    half = iota((256, 128), 1) // 64
    masked = [
        jnp.where(angles == 2 * p + half, doubled, 0.0).astype(BF16) for p in range(4)
    ]
    contrib = mm(jnp.concatenate(masked, axis=1), response_ref[...])
    high = contrib.astype(BF16)
    rest = (contrib - high.astype(F32)).astype(BF16)
    stacked = jnp.concatenate(
        [
            jnp.concatenate(
                [high[:, 128 * p : 128 * p + 128], rest[:, 128 * p : 128 * p + 128]], axis=1
            )
            for p in range(8)
        ],
        axis=0,
    )
    sums = mm(chosen, stacked)
    sums = sums[:, :128] + sums[:, 128:]
    tiles = sums[:count] + pltpu.roll(sums[count:], 64, 1)
    top = tiles.astype(BF16)
    if count == 64:
        top = jnp.concatenate([top, (tiles - top.astype(F32)).astype(BF16)], axis=0)
    by_j = mmt(pick_j_ref[...], top).astype(BF16)
    wide = jnp.concatenate([by_j[16 * i : 16 * i + 16] for i in range(4)], axis=1)
    return mm(wide, spread_x_ref[...])


def gather_view(source, slots, member, sems, start_only=True):
    copies = []
    for off in range(1, VIEWS):
        copies.append(
            pltpu.make_async_remote_copy(
                src_ref=source,
                dst_ref=slots.at[member],
                send_sem=sems.at[0, off],
                recv_sem=sems.at[1, off],
                device_id={"view": lax.rem(member + off, VIEWS)},
                device_id_type=MESH,
            )
        )
    for copy in copies:
        copy.start()
    return copies


def wait_all(copies):
    for copy in copies:
        copy.wait()


def greet(peers):
    barrier = pltpu.get_barrier_semaphore()
    for peer in peers:
        pl.semaphore_signal(barrier, inc=1, device_id=peer, device_id_type=MESH)
    pl.semaphore_wait(barrier, len(peers))


def ahead_kernel(
    volume_ref,
    upstream_ref,
    measured_ref,
    gain_ref,
    pattern_ref,
    angle_ref,
    response_ref,
    pick_x_ref,
    place_ref,
    pick_j_ref,
    spread_x_ref,
    fields_ref,
    ups,
    slots,
    rows,
    gather_sems,
    slab_sems,
):
    slab, member = lax.axis_index("slab"), lax.axis_index("view")
    above, below = lax.rem(slab + 1, SLABS), lax.rem(slab + SLABS - 1, SLABS)
    ups[...] = upstream_ref[...].astype(F32)
    slots[0, member] = volume_ref[...]
    slots[1, member] = ups[...]
    greet(
        [{"view": lax.rem(member + off, VIEWS)} for off in range(1, VIEWS)]
        + [{"slab": above}, {"slab": below}]
    )
    volume_copies = gather_view(volume_ref, slots.at[0], member, gather_sems.at[0])
    ups_copies = gather_view(ups, slots.at[1], member, gather_sems.at[1])
    choice, angles = view_choice(pattern_ref, angle_ref, member)
    wait_all(volume_copies)
    field_rows = slots[0].reshape(128, 128).astype(BF16)
    lines = project(field_rows, choice, angles, response_ref, pick_x_ref, place_ref)
    dual = (gain_ref[...] * (lines - measured_ref[...])).astype(BF16)
    rows[member] = dual
    dual_copies = gather_view(rows.at[member], rows, member, gather_sems.at[2])

    def to_slabs(field):
        copies = []
        for side, peer, start in ((0, above, 0), (1, below, 8)):
            copies.append(
                pltpu.make_async_remote_copy(
                    src_ref=fields_ref.at[field, pl.ds(4, 4)],
                    dst_ref=fields_ref.at[field, pl.ds(start, 4)],
                    send_sem=slab_sems.at[0, field, side],
                    recv_sem=slab_sems.at[1, field, side],
                    device_id={"slab": peer},
                    device_id_type=MESH,
                )
            )
        for copy in copies:
            copy.start()
        return copies

    wait_all(ups_copies)
    left, right = lax.rem(member + VIEWS - 1, VIEWS), lax.rem(member + 1, VIEWS)
    for field in range(2):
        fields_ref[field, 4:8, 4:12, :] = slots[field, member]
        fields_ref[field, 4:8, 0:4, :] = slots[field, left, :, 4:8, :]
        fields_ref[field, 4:8, 12:16, :] = slots[field, right, :, 0:4, :]
    plane_copies = to_slabs(0) + to_slabs(1)
    chosen, columns = band_choice(pattern_ref, angle_ref, 64 * member - 32, 128)
    wait_all(dual_copies)
    spread = backproject(rows, chosen, columns, response_ref, pick_j_ref, spread_x_ref, 128)
    for z in range(4):
        for yt in range(4):
            fields_ref[2, 4 + z, 4 * yt : 4 * yt + 4, :] = spread[
                4 * z : 4 * z + 4, 128 * yt : 128 * yt + 128
            ]
    back_copies = to_slabs(2)
    wait_all(plane_copies)
    wait_all(back_copies)


def shifted(value, e, lane):
    if e == 1:
        return value
    if e == 0:
        return jnp.where(lane == 0, 0.0, pltpu.roll(value, 1, 1))
    return jnp.where(lane == 127, 0.0, pltpu.roll(value, 127, 1))


def conv_kernel(
    fields_ref,
    w1_ref,
    bias1_ref,
    w2_ref,
    bias2_ref,
    w3_ref,
    band1_ref,
    band3_ref,
    rep3_ref,
    fold1_ref,
    fold3_ref,
    new_ref,
    back_ref,
    sums_ref,
    ins,
    ups,
    ups_own,
    t1,
    t3t,
    t3,
    t1t,
    w2r,
    w2t,
    pre1,
    h3,
    ct3,
    h2,
    s3,
    s2z,
    s1,
    g2,
    g3,
):
    slab, member = lax.axis_index("slab"), lax.axis_index("view")
    low_z, low_y = 4 * slab - 4, 8 * member - 4
    depth, height = 4 * SLABS, 8 * VIEWS

    base = jnp.zeros((32, 384), F32)
    for tap in range(9):
        base = base + mm(w1_ref[tap], band1_ref[tap])
    for yo in range(14):
        t1[32 * yo : 32 * yo + 32, :] = (pltpu.roll(base, yo, 1) if yo else base).astype(BF16)
    eye96 = one(iota((96, 96), 0) == iota((96, 96), 1))
    w3 = w3_ref[...]
    w3_turned = mmt(eye96, w3).astype(BF16)
    base3 = jnp.zeros((32, 256), F32)
    for e in range(3):
        base3 = base3 + mm(w3_turned[32 * (2 - e) : 32 * (2 - e) + 32], band3_ref[e])
    for yo in range(12):
        t3t[32 * yo : 32 * yo + 32, :] = pltpu.roll(base3, yo + 1, 1).astype(BF16)
    step = iota((8, 384), 1) // 32 - iota((8, 384), 0)
    for e in range(3):
        line = mm(w3, rep3_ref[e])
        for a in range(3):
            block = jnp.zeros((8, 384), F32)
            for b in range(3):
                block = block + jnp.where(step == b, line[3 * a + b : 3 * a + b + 1, :], 0.0)
            t3[8 * (3 * a + e) : 8 * (3 * a + e) + 8, :] = block
    eye6 = one(iota((8, 6), 0) == iota((8, 6), 1))
    turned = [
        mmt(eye6, jnp.concatenate([w1_ref[tap]] * 12, axis=0)) for tap in range(9)
    ]
    for a in range(3):
        for c in range(2):
            for e in range(3):
                row = 2 * (2 - e) + c
                block = jnp.zeros((8, 384), F32)
                for b in range(3):
                    tap = 3 * (2 - a) + (2 - b)
                    block = block + jnp.where(step == b, turned[tap][row : row + 1, :], 0.0)
                at = 8 * ((a * 2 + c) * 3 + e)
                t1t[at : at + 8, :] = block
    wide = mm(
        jnp.concatenate([w2_ref[tap] for tap in range(9)], axis=0),
        one(iota((96, 128), 0) == iota((96, 128), 1)),
    )
    keep = iota((128, 128), 1) // 32 == 2 - iota((128, 128), 0) // 32
    towers = []
    for tap in range(9):
        piece = wide[32 * tap : 32 * tap + 32]
        a, b = tap // 3, tap % 3
        w2r[32 * a : 32 * a + 32, 128 * b : 128 * b + 128] = piece.astype(BF16)
        towers.append(
            jnp.where(keep, jnp.concatenate([piece] * 4, axis=0), 0.0).astype(BF16)
        )
    across = mmt(
        one(iota((32, 128), 0) == iota((32, 128), 1) % 32), jnp.concatenate(towers, axis=0)
    ).astype(BF16)
    for a in range(3):
        for b in range(3):
            tap = 3 * (2 - a) + (2 - b)
            w2t[32 * a : 32 * a + 32, 128 * b : 128 * b + 128] = across[
                :, 128 * tap : 128 * tap + 128
            ]
    eye32 = iota((32, 32), 0) == iota((32, 32), 1)
    bias1 = jnp.sum(jnp.where(eye32, bias1_ref[...], 0.0), axis=1, keepdims=True)
    bias2 = jnp.sum(jnp.where(eye32, bias2_ref[...], 0.0), axis=1, keepdims=True)

    lane16 = iota((16, 128), 1)
    global_y = iota((16, 128), 0) + low_y
    inside_y = (global_y >= 0) & (global_y < height)
    lane8 = iota((8, 128), 1)

    def prepare(z, carry):
        inside = inside_y & (z + low_z >= 0) & (z + low_z < depth)
        for c, field in ((0, 0), (1, 2)):
            plane = jnp.where(inside, fields_ref[field, z], 0.0)
            plane = plane.astype(BF16).astype(F32)
            for e in range(3):
                at = (c * 3 + e) * 16
                ins[z, at : at + 16, :] = shifted(plane, e, lane16).astype(BF16)
        plane = jnp.where(inside, fields_ref[1, z], 0.0)
        for e in range(3):
            ups[z, 16 * e : 16 * e + 16, :] = shifted(plane, e, lane16).astype(BF16)
        return carry

    lax.fori_loop(0, 12, prepare, 0)
    ups_own[...] = jnp.zeros(ups_own.shape, F32)
    for z in range(4):
        plane = fields_ref[1, 4 + z, 4:12, :]
        for e in range(3):
            ups_own[2 + z, e] = shifted(plane, 2 - e, lane8)

    def pair_of(ref, z, count):
        cols = [
            jnp.concatenate([ref[z + n + a] for a in range(count)], axis=0) for n in range(2)
        ]
        return jnp.concatenate(cols, axis=1)

    def first(p, carry):
        z = 2 * p
        out = mm(t1[:, :288], pair_of(ins, z, 3))
        pre1[z] = out[:, :128]
        pre1[z + 1] = out[:, 128:]
        return carry

    lax.fori_loop(0, 5, first, 0)

    lane448 = iota((448, 128), 1)
    row_y1 = iota((448, 128), 0) // 32 + low_y + 1
    inside1 = (row_y1 >= 0) & (row_y1 < height)
    bias1_rows = jnp.concatenate([jnp.broadcast_to(bias1, (32, 128))] * 14, axis=0)

    def activate(z, carry):
        value = pre1[z] + bias1_rows
        gate = 0.5 * jnp.tanh(0.5 * value) + 0.5
        act = value * gate
        pre1[z] = gate + act * (1.0 - gate)
        inside = inside1 & (z + low_z + 1 >= 0) & (z + low_z + 1 < depth)
        act = jnp.where(inside, act, 0.0)
        for e in range(3):
            h3[z, :, 32 * e : 32 * e + 32, :] = (
                shifted(act, e, lane448).astype(BF16).reshape(14, 32, 128)
            )
        h3[z, :, 96:128, :] = jnp.ones((14, 32, 128), BF16)
        return carry

    lax.fori_loop(0, 10, activate, 0)

    def third_turned(p, carry):
        z = 2 * p
        out = mm(t3t[:, :144], pair_of(ups, z + 1, 3))
        ct3[z] = out[:, :128]
        ct3[z + 1] = out[:, 128:]
        return carry

    lax.fori_loop(0, 4, third_turned, 0)

    lane32 = iota((32, 128), 1)
    s2z[...] = jnp.zeros(s2z.shape, BF16)

    def stacked_rows(ref, z, y):
        cols = [ref[z + n, pl.ds(y, 3)].reshape(384, 128) for n in range(2)]
        return jnp.concatenate(cols, axis=1)

    def second(y, carry):
        outs = [mm(w2r[...], stacked_rows(h3, 2 * p, y)) for p in range(5)]
        parts = [outs[z // 2][:, 128 * (z % 2) : 128 * (z % 2) + 128] for z in range(10)]
        ok_y = (y + low_y + 2 >= 0) & (y + low_y + 2 < height)
        at = pl.multiple_of(32 * y, 32)
        for z in range(8):
            value = parts[z][:32] + parts[z + 1][32:64] + parts[z + 2][64:] + bias2
            gate = 0.5 * jnp.tanh(0.5 * value) + 0.5
            act = value * gate
            slope = gate + act * (1.0 - gate)
            ok = ok_y & (z + low_z + 2 >= 0) & (z + low_z + 2 < depth)
            live = jnp.where(ok, 1.0, 0.0)
            h2[z, pl.ds(at, 32), :] = (act * live).astype(BF16)
            slope = slope * ct3[z, pl.ds(at, 32), :] * live
            for e in range(3):
                s3[z, y, 32 * e : 32 * e + 32, :] = shifted(slope, e, lane32).astype(BF16)
            s3[z, y, 96:128, :] = jnp.zeros((32, 128), BF16)
        return carry

    lax.fori_loop(0, 12, second, 0)
    for z in range(2, 6):
        s2z[z] = s3[z, 2:10, 32:64, :]

    g2[...] = jnp.zeros(g2.shape, F32)

    def second_grad(y, carry):
        left = jnp.concatenate(
            [
                jnp.concatenate([s2z[z - a, y] for z in range(2, 8)], axis=1)
                for a in range(3)
            ],
            axis=0,
        )
        right = jnp.concatenate(
            [h3[z, pl.ds(y + 2, 3)].reshape(384, 128) for z in range(2, 8)], axis=1
        )
        g2[...] += mmt(left, right)
        return carry

    lax.fori_loop(0, 8, second_grad, 0)

    def second_turned(y, carry):
        outs = [mm(w2t[...], stacked_rows(s3, 2 * p, y)) for p in range(4)]
        parts = [outs[z // 2][:, 128 * (z % 2) : 128 * (z % 2) + 128] for z in range(8)]
        ok_y = (y + low_y + 3 >= 0) & (y + low_y + 3 < height)
        at = pl.multiple_of(32 * y, 32)
        from_ = pl.multiple_of(32 * y + 64, 32)
        for z in range(6):
            value = parts[z][:32] + parts[z + 1][32:64] + parts[z + 2][64:]
            ok = ok_y & (z + low_z + 3 >= 0) & (z + low_z + 3 < depth)
            live = jnp.where(ok, 1.0, 0.0)
            value = value * pre1[z + 2, pl.ds(from_, 32), :] * live
            s1[z, pl.ds(at, 32), :] = value.astype(BF16)
        return carry

    lax.fori_loop(0, 10, second_turned, 0)

    t1t_now = t1t[:, :320].astype(BF16)
    outs = [mm(t1t_now, jnp.concatenate([s1[2 * p], s1[2 * p + 1]], axis=1)) for p in range(3)]
    for c in range(2):
        for z in range(4):
            for e in range(3):
                total = jnp.zeros((8, 128), F32)
                for a in range(3):
                    zi = z + a
                    at = 8 * ((a * 2 + c) * 3 + e)
                    total = total + outs[zi // 2][
                        at : at + 8, 128 * (zi % 2) : 128 * (zi % 2) + 128
                    ]
                total = shifted(total, e, lane8)
                if e == 0:
                    back_ref[c, z] = total
                else:
                    back_ref[c, z] += total

    t3_now = t3[:, :320].astype(BF16)
    outs = [
        mm(t3_now, jnp.concatenate([h2[z, 32:352, :], h2[z + 1, 32:352, :]], axis=1))
        for z in (1, 3, 5)
    ]
    for z in range(4):
        total = fields_ref[0, 4 + z, 4:12, :]
        for e in range(3):
            part = jnp.zeros((8, 128), F32)
            for a in range(3):
                zi = z + a
                at = 8 * (3 * a + e)
                part = part + outs[zi // 2][at : at + 8, 128 * (zi % 2) : 128 * (zi % 2) + 128]
            total = total + shifted(part, e, lane8)
        new_ref[z] = total

    left = jnp.concatenate(
        [
            jnp.concatenate(
                [ups_own[z + 1 - a, e] for a in range(3) for e in range(3)], axis=0
            ).astype(BF16)
            for z in range(1, 7)
        ],
        axis=1,
    )
    right = jnp.concatenate([h2[z, 32:352, :] for z in range(1, 7)], axis=1)
    cross = mmt(left, right)
    step10 = iota((8, 320), 1) // 32 - iota((8, 320), 0)
    g3[...] = jnp.zeros(g3.shape, F32)
    for a in range(3):
        for e in range(3):
            block = cross[8 * (3 * a + e) : 8 * (3 * a + e) + 8]
            for b in range(3):
                g3[e, 3 * a + b : 3 * a + b + 1, 0:320] = jnp.sum(
                    jnp.where(step10 == b, block, 0.0), axis=0, keepdims=True
                )
    third = jnp.zeros((16, 128), F32)
    for e in range(3):
        value = g3[e]
        high = value.astype(BF16)
        rest = (value - high.astype(F32)).astype(BF16)
        third = third + mm(high, fold3_ref[e]) + mm(rest, fold3_ref[e])

    left = jnp.concatenate([s1[z, 32:288, :] for z in range(1, 5)], axis=1)
    right = jnp.concatenate(
        [
            jnp.concatenate(
                [ins[z + 3 + a] for a in range(3)] + [jnp.ones((96, 128), BF16)], axis=0
            )
            for z in range(4)
        ],
        axis=1,
    )
    cross = mmt(left, right)
    total = cross[:32]
    for yo in range(1, 8):
        total = total + pltpu.roll(cross[32 * yo : 32 * yo + 32], 384 - yo, 1)
    high = total.astype(BF16)
    rest = (total - high.astype(F32)).astype(BF16)
    first_grads = mm(high, fold1_ref[...]) + mm(rest, fold1_ref[...])

    lane_keep = iota((32, 128), 1) < 97
    for tap in range(9):
        a, b = tap // 3, tap % 3
        block = jnp.where(
            lane_keep, g2[32 * a : 32 * a + 32, 128 * b : 128 * b + 128], 0.0
        ) + first_grads[:, 128 * tap : 128 * tap + 128]
        sums_ref[4 * tap : 4 * tap + 4] = block.reshape(4, 8, 128)
    sums_ref[36:38] = third.reshape(2, 8, 128)
    sums_ref[38:40] = jnp.zeros((2, 8, 128), F32)


def behind_kernel(
    back_ref,
    upstream_ref,
    gain_ref,
    pattern_ref,
    angle_ref,
    response_ref,
    pick_x_ref,
    place_ref,
    pick_j_ref,
    spread_x_ref,
    sums_ref,
    grad_ref,
    total_ref,
    slots,
    rows,
    ring_in,
    view_in,
    layer_in,
    gather_sems,
    ring_sems,
    view_sems,
    layer_sems,
    final_sems,
):
    slab, member = lax.axis_index("slab"), lax.axis_index("view")
    place, layer = lax.rem(slab, RING), lax.div(slab, RING)
    ring_peers = [layer * RING + lax.rem(place + off, RING) for off in range(1, RING)]
    layer_peers = [
        lax.rem(layer + off, LAYERS) * RING + place for off in range(1, LAYERS)
    ]
    slots[member] = back_ref[1]
    greet(
        [{"view": lax.rem(member + off, VIEWS)} for off in range(1, VIEWS)]
        + [{"slab": peer} for peer in ring_peers]
        + [{"slab": peer} for peer in layer_peers]
    )
    field_copies = gather_view(back_ref.at[1], slots, member, gather_sems.at[0])

    def to_peers(source_of, target, axis, peers, sems):
        copies = []
        for n, peer in enumerate(peers):
            copies.append(
                pltpu.make_async_remote_copy(
                    src_ref=source_of(n),
                    dst_ref=target,
                    send_sem=sems.at[0, n],
                    recv_sem=sems.at[1, n],
                    device_id={axis: peer},
                    device_id_type=MESH,
                )
            )
        for copy in copies:
            copy.start()
        return copies

    ring_copies = to_peers(
        lambda n: sums_ref.at[pl.ds(PIECE * lax.rem(place + n + 1, RING), PIECE)],
        ring_in.at[place],
        "slab",
        ring_peers,
        ring_sems,
    )
    ring_in[place] = sums_ref[pl.ds(PIECE * place, PIECE)]
    choice, angles = view_choice(pattern_ref, angle_ref, member)
    wait_all(field_copies)
    field_rows = slots[...].reshape(128, 128).astype(BF16)
    lines = project(field_rows, choice, angles, response_ref, pick_x_ref, place_ref)
    rows[member] = (gain_ref[...] * lines).astype(BF16)
    echo_copies = gather_view(rows.at[member], rows, member, gather_sems.at[1])

    def add_up(ref, count):
        total = ref[0]
        for n in range(1, count):
            total = total + ref[n]
        return total

    wait_all(ring_copies)
    view_in[member] = add_up(ring_in, RING)
    view_copies = to_peers(
        lambda n: view_in.at[member],
        view_in.at[member],
        "view",
        [lax.rem(member + off, VIEWS) for off in range(1, VIEWS)],
        view_sems,
    )
    chosen, columns = band_choice(pattern_ref, angle_ref, 64 * member, 64)
    wait_all(view_copies)
    layer_in[layer] = add_up(view_in, VIEWS)
    layer_copies = to_peers(
        lambda n: layer_in.at[layer], layer_in.at[layer], "slab", layer_peers, layer_sems
    )
    wait_all(echo_copies)
    spread = backproject(rows, chosen, columns, response_ref, pick_j_ref, spread_x_ref, 64)
    spread = spread[:, :256] + spread[:, 256:]
    wait_all(layer_copies)
    total_ref[pl.ds(PIECE * place, PIECE)] = add_up(layer_in, LAYERS)
    final_copies = to_peers(
        lambda n: total_ref.at[pl.ds(PIECE * place, PIECE)],
        total_ref.at[pl.ds(PIECE * place, PIECE)],
        "slab",
        ring_peers,
        final_sems,
    )
    base = upstream_ref[...].astype(F32) + back_ref[0]
    for z in range(4):
        for yt in range(2):
            grad_ref[z, 4 * yt : 4 * yt + 4, :] = (
                base[z, 4 * yt : 4 * yt + 4, :]
                + spread[4 * z : 4 * z + 4, 128 * yt : 128 * yt + 128]
            )
    wait_all(final_copies)


def vmem_specs(count):
    return [pl.BlockSpec(memory_space=pltpu.VMEM)] * count


def body(volume, measured, dual_gain, pattern, angle, response, w1, bias1, w2, bias2, w3, upstream):
    measured2 = measured.reshape(32, 128)
    gain2 = dual_gain.reshape(32, 128)
    pattern3 = pattern.reshape(VIEWS, 64, 16)
    angle2 = angle.reshape(VIEWS, 64)
    moves = [jnp.asarray(x) for x in tile_constants()]
    dma = pltpu.SemaphoreType.DMA
    fields = pl.pallas_call(
        ahead_kernel,
        name="ahead",
        out_shape=jax.ShapeDtypeStruct((3, 12, 16, 128), F32),
        in_specs=vmem_specs(11),
        out_specs=vmem_specs(1)[0],
        scratch_shapes=[
            pltpu.VMEM((4, 8, 128), F32),
            pltpu.VMEM((2, VIEWS, 4, 8, 128), F32),
            pltpu.VMEM((VIEWS, 32, 128), BF16),
            dma((3, 2, VIEWS)),
            dma((2, 3, 2)),
        ],
        compiler_params=pltpu.CompilerParams(
            collective_id=0, has_side_effects=True, vmem_limit_bytes=VMEM_BYTES
        ),
    )(volume, upstream, measured2, gain2, pattern3, angle2, response, *moves)

    consts = [jnp.asarray(x) for x in weight_constants()]
    new_volume, back, sums = pl.pallas_call(
        conv_kernel,
        name="convs",
        out_shape=(
            jax.ShapeDtypeStruct((4, 8, 128), F32),
            jax.ShapeDtypeStruct((2, 4, 8, 128), F32),
            jax.ShapeDtypeStruct((PIECE * RING, 8, 128), F32),
        ),
        in_specs=vmem_specs(11),
        out_specs=tuple(vmem_specs(3)),
        scratch_shapes=[
            pltpu.VMEM((12, 96, 128), BF16),
            pltpu.VMEM((12, 48, 128), BF16),
            pltpu.VMEM((8, 3, 8, 128), F32),
            pltpu.VMEM((448, 384), BF16),
            pltpu.VMEM((384, 256), BF16),
            pltpu.VMEM((72, 384), F32),
            pltpu.VMEM((144, 384), F32),
            pltpu.VMEM((96, 384), BF16),
            pltpu.VMEM((96, 384), BF16),
            pltpu.VMEM((10, 448, 128), F32),
            pltpu.VMEM((10, 14, 128, 128), BF16),
            pltpu.VMEM((8, 384, 128), F32),
            pltpu.VMEM((8, 384, 128), BF16),
            pltpu.VMEM((8, 12, 128, 128), BF16),
            pltpu.VMEM((8, 8, 32, 128), BF16),
            pltpu.VMEM((6, 320, 128), BF16),
            pltpu.VMEM((96, 384), F32),
            pltpu.VMEM((3, 16, 384), F32),
        ],
        compiler_params=pltpu.CompilerParams(vmem_limit_bytes=VMEM_BYTES),
    )(fields, w1, bias1.reshape(1, 32), w2, bias2.reshape(1, 32), w3.reshape(9, 96), *consts)

    grad_volume, total = pl.pallas_call(
        behind_kernel,
        name="behind",
        out_shape=(
            jax.ShapeDtypeStruct((4, 8, 128), F32),
            jax.ShapeDtypeStruct((PIECE * RING, 8, 128), F32),
        ),
        in_specs=vmem_specs(11),
        out_specs=tuple(vmem_specs(2)),
        scratch_shapes=[
            pltpu.VMEM((VIEWS, 4, 8, 128), F32),
            pltpu.VMEM((VIEWS, 32, 128), BF16),
            pltpu.VMEM((RING, PIECE, 8, 128), F32),
            pltpu.VMEM((VIEWS, PIECE, 8, 128), F32),
            pltpu.VMEM((LAYERS, PIECE, 8, 128), F32),
            dma((2, 2, VIEWS)),
            dma((2, RING - 1)),
            dma((2, VIEWS - 1)),
            dma((2, LAYERS - 1)),
            dma((2, RING - 1)),
        ],
        compiler_params=pltpu.CompilerParams(
            collective_id=1, has_side_effects=True, vmem_limit_bytes=VMEM_BYTES
        ),
    )(back, upstream, gain2, pattern3, angle2, response, *moves, sums)

    scale = 1.0 / math.sqrt(volume.size * SLABS * VIEWS)
    scaled = total.reshape(PIECE * RING * 8, 128) * scale
    taps = scaled[:288].reshape(9, 32, 128)
    return (
        new_volume,
        grad_volume,
        taps[:, :, 97:103],
        taps[0, :, 103],
        taps[:, :, :96],
        taps[4, :, 96],
        scaled[288:297, :96].reshape(9, 1, 96),
    )


def solution(mesh):
    placed = (
        P("slab", "view", None),
        P("view", "slab", None),
        P("view", "slab", None),
        P(None, "slab", None, None),
        P(None, "slab", None),
        P(),
        P(),
        P(),
        P(),
        P(),
        P(),
        P("slab", "view", None),
    )
    return jax.shard_map(
        body,
        mesh=mesh,
        in_specs=placed,
        out_specs=(P("slab", "view", None), P("slab", "view", None), P(), P(), P(), P(), P()),
        check_vma=False,
    )
```

time: 533 us -> 69.8 us (0.13)
  the two profiles are of different devices: /device:TPU:31 before, /device:TPU:0 now
where the time goes in v1:
time: 69.8 us; the launch traced here: 69.5 us
  Pallas kernels  60.6 us (87%)
  local copies, waits for them, and re-layouts  7.93 us (11%)
  between operations  0.92 us (1%)
    pallas_call x1, Pallas kernels, body(): pl.pallas_call(ahead_kernel, name='ahead', out_shape=jax.ShapeDtypeStruct...  21.6 us
    pallas_call x1, Pallas kernels, body(): pl.pallas_call(behind_kernel, name='behind', out_shape=(jax.ShapeDtypeStr...  20.3 us
    pallas_call x1, Pallas kernels, body(): pl.pallas_call(conv_kernel, name='convs', out_shape=(jax.ShapeDtypeStruct...  18.7 us
    unnamed x52, local copies, waits for them, and re-layouts  6.52 us

profile of v1, /device:TPU:0, one launch (start us, length us, event | category | flops | bytes accessed | tf_op | source)
XLA Modules:
  0.0 69.5 jit_solution(10443308914118031366)
XLA Ops:
  0.6 0.0 copy-start.23
  0.6 0.9 %copy.32.w1_ref = bf16[9,32,6]{2,1,0:T(8,128)(2,1)S(1)} copy(bf16[9,32,6]{1,2,0:T(8,128)(2,1)} %param.27) | data formatting | bytes 6912 | tf_op args[6]
  1.5 0.0 copy-done.23
  1.5 0.0 copy-start.9
  1.5 0.0 copy-start.11
  1.5 0.0 copy-start.12
  1.6 0.0 copy-start.14
  1.6 0.0 copy-start.16
  1.6 0.0 copy-start.17
  1.6 0.0 copy-start.18
  1.6 0.1 copy.31
  1.7 0.6 copy-done.9
  2.3 0.0 copy-done.11
  2.3 0.0 copy-done.12
  2.3 0.0 copy-done.14
  2.3 0.0 copy-done.16
  2.3 0.0 copy-done.17
  2.3 0.0 copy-done.18
  2.3 0.0 copy-start
  2.3 1.2 %copy-done = bf16[512,1024]{1,0:T(8,128)(2,1)S(1)} copy-done((bf16[512,1024]{1,0:T(8,128)(2,1)S(1)}, bf16[512,1024]{1,0:T(8,128)(2,1)}, u32[]{:S(2)}) %copy-start) | copy-done | bytes 1048600
  3.6 0.0 copy-start.2
  3.6 1.2 %copy-done.2 = bf16[512,1024]{1,0:T(8,128)(2,1)S(1)} copy-done((bf16[512,1024]{1,0:T(8,128)(2,1)S(1)}, bf16[512,1024]{1,0:T(8,128)(2,1)}, u32[]{:S(2)}) %copy-start.2) | copy-done | bytes 1048600
  4.8 0.0 copy-start.4
  4.8 1.0 %copy-done.4 = bf16[512,512]{1,0:T(8,128)(2,1)S(1)} copy-done((bf16[512,512]{1,0:T(8,128)(2,1)S(1)}, bf16[512,512]{1,0:T(8,128)(2,1)}, u32[]{:S(2)}) %copy-start.4) | copy-done | bytes 524312
  5.8 0.0 copy-start.6
  5.8 0.0 copy-start.7
  5.8 0.0 copy-start.8
  5.8 0.0 copy-start.10
  5.8 0.0 copy-start.13
  5.8 0.0 copy-start.15
  5.9 0.0 copy-start.19
  5.9 0.0 copy-start.20
  5.9 0.0 copy-start.21
  5.9 0.0 copy-start.3
  5.9 21.6 %ahead.1.fields_ref = f32[3,12,16,128]{3,2,1,0:T(8,128)S(1)} custom-call(f32[4,8,128]{2,1,0:T(8,128)S(1)} %copy-done.16, bf16[4,8,128]{2,1,0:T(8,128)(2,1)S(1)} %copy-done.14, f32[32,128]{1,0:T(8,128)S(1)} %bitcast.15, f32[32,128]{1,0:T(8,128)S(1)} %bitcast.13, s32[4,64,16]{2,1,0:T(8,128)S(1)} %bitcast.11, s32[4,64]{1,0:T(4,128)S(1)} %bitcast.16, ...), custom_call_target="tpu_custom_call" | custom-call | tf_op jit(solution)/shard_map/ahead/pallas_call | solution.py:738
  27.6 0.0 copy-done.6
  27.6 0.0 copy-done.7
  27.6 0.0 copy-done.8
  27.6 0.0 copy-done.10
  27.6 0.0 copy-done.13
  27.6 0.0 copy-done.15
  27.6 0.0 copy-done.19
  27.6 0.0 copy-done.20
  27.6 0.0 copy-done.21
  27.6 0.0 copy-start.1
  27.7 0.0 copy-start.5
  27.7 18.7 %convs.1 = (f32[4,8,128]{2,1,0:T(8,128)}, f32[2,4,8,128]{3,2,1,0:T(8,128)S(1)}, f32[40,8,128]{2,1,0:T(8,128)S(1)}) custom-call(f32[3,12,16,128]{3,2,1,0:T(8,128)S(1)} %ahead.1.fields_ref, bf16[9,32,6]{2,1,0:T(8,128)(2,1)S(1)} %copy.32.w1_ref, f32[1,32]{1,0:T(1,128)S(1)} %bitcast.19, bf16[9,32,96]{2,1,0:T(8,128)(2,1)S(1)} %copy-done.10, ...), custom_call_target="tpu_custom_call" | custom-call | tf_op jit(solution)/shard_map/convs/pallas_call | solution.py:757
  46.3 0.0 copy-done.3
  46.3 0.0 copy-done.1
  46.3 0.0 copy-done.5
  46.4 20.3 %behind.1 = (f32[4,8,128]{2,1,0:T(8,128)S(1)}, f32[40,8,128]{2,1,0:T(8,128)S(1)}) custom-call(f32[2,4,8,128]{3,2,1,0:T(8,128)S(1)} %get-tuple-element.13.back_ref, bf16[4,8,128]{2,1,0:T(8,128)(2,1)S(1)} %copy-done.14, f32[32,128]{1,0:T(8,128)S(1)} %bitcast.14, s32[4,64,16]{2,1,0:T(8,128)S(1)} %bitcast.12, s32[4,64]{1,0:T(4,128)S(1)} %bitcast.17, ...), custom_call_target="tpu_custom_call" | custom-call | tf_op jit(solution)/shard_map/behind/pallas_call | solution.py:790
  66.7 0.6 reshape.54
  67.3 0.0 copy-start.22
  67.3 0.7 %slice_reduce_fusion = (f32[32]{0:T(128)}, f32[32]{0:T(128)}) fusion(f32[9,32,128]{2,1,0:T(8,128)S(1)} %bitcast.21), kind=kLoop, calls=%fused_computation.1 | loop fusion | bytes 512 | tf_op jit(solution)/shard_map/slice | solution.py:825
  68.0 0.1 slice.26
  68.1 0.0 copy-done.22
  68.1 0.7 %copy.33 = f32[9,32,6]{1,2,0:T(8,128)} copy(f32[9,32,6]{2,1,0:T(8,128)S(1)} %slice.26) | data formatting | bytes 13824
  68.9 0.6 copy.35
  (3 shorter events, 0.0 us)
Async XLA Ops:
  0.6 0.9 %copy-start.23 = (s32[4,1,64,16]{2,3,1,0:T(8,128)S(1)}, s32[4,1,64,16]{2,3,1,0:T(8,128)}, u32[]{:S(2)}) copy-start(s32[4,1,64,16]{2,3,1,0:T(8,128)} %param.24) | copy-start | bytes 49156
  1.5 0.8 %copy-start.9 = (bf16[128,128]{1,0:T(8,128)(2,1)S(1)}, bf16[128,128]{1,0:T(8,128)(2,1)}, u32[]{:S(2)}) copy-start(bf16[128,128]{1,0:T(8,128)(2,1)} %constant.20.clone.pick_x_ref) | copy-start | bytes 98308
  1.5 0.8 %copy-start.11 = (f32[1,1,4096]{2,1,0:T(1,128)S(1)}, f32[1,1,4096]{2,1,0:T(1,128)}, u32[]{:S(2)}) copy-start(f32[1,1,4096]{2,1,0:T(1,128)} %param.23) | copy-start | bytes 49156
  1.5 0.7 %copy-start.12 = (bf16[64,128]{1,0:T(8,128)(2,1)S(1)}, bf16[64,128]{1,0:T(8,128)(2,1)}, u32[]{:S(2)}) copy-start(bf16[64,128]{1,0:T(8,128)(2,1)} %constant.22.clone.pick_j_ref) | copy-start | bytes 49156
  1.6 0.7 %copy-start.14 = (bf16[4,8,128]{2,1,0:T(8,128)(2,1)S(1)}, bf16[4,8,128]{2,1,0:T(8,128)(2,1)}, u32[]{:S(2)}) copy-start(bf16[4,8,128]{2,1,0:T(8,128)(2,1)} %upstream_ref.3) | copy-start | bytes 24580
  1.6 0.7 %copy-start.16 = (f32[4,8,128]{2,1,0:T(8,128)S(1)}, f32[4,8,128]{2,1,0:T(8,128)}, u32[]{:S(2)}) copy-start(f32[4,8,128]{2,1,0:T(8,128)} %volume_ref.1) | copy-start | bytes 49156
  1.6 0.7 %copy-start.17 = (f32[1,1,4096]{2,1,0:T(1,128)S(1)}, f32[1,1,4096]{2,1,0:T(1,128)}, u32[]{:S(2)}) copy-start(f32[1,1,4096]{2,1,0:T(1,128)} %param.22) | copy-start | bytes 49156
  1.6 0.7 %copy-start.18 = (s32[4,1,64]{2,1,0:T(1,128)S(1)}, s32[4,1,64]{2,1,0:T(1,128)}, u32[]{:S(2)}) copy-start(s32[4,1,64]{2,1,0:T(1,128)} %param.25) | copy-start | bytes 3076
  2.3 1.2 %copy-start = (bf16[512,1024]{1,0:T(8,128)(2,1)S(1)}, bf16[512,1024]{1,0:T(8,128)(2,1)}, u32[]{:S(2)}) copy-start(bf16[512,1024]{1,0:T(8,128)(2,1)} %response_ref.3) | copy-start | bytes 3145732
  3.6 1.2 %copy-start.2 = (bf16[512,1024]{1,0:T(8,128)(2,1)S(1)}, bf16[512,1024]{1,0:T(8,128)(2,1)}, u32[]{:S(2)}) copy-start(bf16[512,1024]{1,0:T(8,128)(2,1)} %constant.21.clone.place_ref) | copy-start | bytes 3145732
  4.8 1.0 %copy-start.4 = (bf16[512,512]{1,0:T(8,128)(2,1)S(1)}, bf16[512,512]{1,0:T(8,128)(2,1)}, u32[]{:S(2)}) copy-start(bf16[512,512]{1,0:T(8,128)(2,1)} %constant.23.clone.spread_x_ref) | copy-start | bytes 1572868
  5.8 21.7 %copy-start.6 = (bf16[384,1152]{1,0:T(8,128)(2,1)S(1)}, bf16[384,1152]{1,0:T(8,128)(2,1)}, u32[]{:S(2)}) copy-start(bf16[384,1152]{1,0:T(8,128)(2,1)} %constant.27.clone.fold1_ref) | copy-start | bytes 2654212
  5.8 21.7 %copy-start.7 = (bf16[3,384,128]{2,1,0:T(8,128)(2,1)S(1)}, bf16[3,384,128]{2,1,0:T(8,128)(2,1)}, u32[]{:S(2)}) copy-start(bf16[3,384,128]{2,1,0:T(8,128)(2,1)} %constant.28.clone.fold3_ref) | copy-start | bytes 884740
  5.8 21.8 %copy-start.8 = (bf16[3,96,384]{2,1,0:T(8,128)(2,1)S(1)}, bf16[3,96,384]{2,1,0:T(8,128)(2,1)}, u32[]{:S(2)}) copy-start(bf16[3,96,384]{2,1,0:T(8,128)(2,1)} %constant.26.clone.rep3_ref) | copy-start | bytes 663556
  5.8 21.8 %copy-start.10 = (bf16[9,32,96]{2,1,0:T(8,128)(2,1)S(1)}, bf16[9,32,96]{2,1,0:T(8,128)(2,1)}, u32[]{:S(2)}) copy-start(bf16[9,32,96]{2,1,0:T(8,128)(2,1)} %w2_ref.1) | copy-start | bytes 165892
  5.8 21.8 %copy-start.13 = (bf16[9,6,384]{2,1,0:T(8,128)(2,1)S(1)}, bf16[9,6,384]{2,1,0:T(8,128)(2,1)}, u32[]{:S(2)}) copy-start(bf16[9,6,384]{2,1,0:T(8,128)(2,1)} %constant.24.clone.band1_ref) | copy-start | bytes 124420
  5.8 21.8 %copy-start.15 = (bf16[3,9,256]{2,1,0:T(8,128)(2,1)S(1)}, bf16[3,9,256]{2,1,0:T(8,128)(2,1)}, u32[]{:S(2)}) copy-start(bf16[3,9,256]{2,1,0:T(8,128)(2,1)} %constant.25.clone.band3_ref) | copy-start | bytes 41476
  5.9 21.8 %copy-start.19 = (bf16[9,1,96]{2,0,1:T(8,128)(2,1)S(1)}, bf16[9,1,96]{2,0,1:T(8,128)(2,1)}, u32[]{:S(2)}) copy-start(bf16[9,1,96]{2,0,1:T(8,128)(2,1)} %param.31) | copy-start | bytes 5188
  5.9 21.8 %copy-start.20 = (f32[32]{0:T(128)S(1)}, f32[32]{0:T(128)}, u32[]{:S(2)}) copy-start(f32[32]{0:T(128)} %param.28) | copy-start | bytes 388
  5.9 21.8 %copy-start.21 = (f32[32]{0:T(128)S(1)}, f32[32]{0:T(128)}, u32[]{:S(2)}) copy-start(f32[32]{0:T(128)} %param.30) | copy-start | bytes 388
  5.9 40.5 %copy-start.3 = (bf16[512,1024]{1,0:T(8,128)(2,1)S(1)}, bf16[512,1024]{1,0:T(8,128)(2,1)}, u32[]{:S(2)}) copy-start(bf16[512,1024]{1,0:T(8,128)(2,1)} %constant.21.clone.place_ref) | copy-start | bytes 3145732
  27.6 18.7 %copy-start.1 = (bf16[512,1024]{1,0:T(8,128)(2,1)S(1)}, bf16[512,1024]{1,0:T(8,128)(2,1)}, u32[]{:S(2)}) copy-start(bf16[512,1024]{1,0:T(8,128)(2,1)} %response_ref.3) | copy-start | bytes 3145732
  27.7 18.7 %copy-start.5 = (bf16[512,512]{1,0:T(8,128)(2,1)S(1)}, bf16[512,512]{1,0:T(8,128)(2,1)}, u32[]{:S(2)}) copy-start(bf16[512,512]{1,0:T(8,128)(2,1)} %constant.23.clone.spread_x_ref) | copy-start | bytes 1572868
  67.3 0.8 %copy-start.22 = (f32[36,8,128]{2,1,0:T(8,128)}, f32[36,8,128]{2,1,0:T(8,128)S(1)}, u32[]{:S(2)}) copy-start(f32[36,8,128]{2,1,0:T(8,128)S(1)} %slice.25) | copy-start | bytes 442372

commit v2 on v0

v2 whole, which is shorter than its diff:
```python
import functools
import math

import jax
import jax.numpy as jnp
import ml_dtypes
import numpy as np
from jax import lax
from jax.experimental import pallas as pl
from jax.experimental.pallas import tpu as pltpu
from jax.sharding import PartitionSpec as P

F32 = jnp.float32
BF16 = jnp.bfloat16
MESH = pl.DeviceIdType.MESH
VIEWS = 4
RING = 8
LAYERS = 4
SLABS = RING * LAYERS
PIECE = 5
VMEM_BYTES = 56 * 1024 * 1024
HELD = pl.ANY


def mm(a, b):
    return lax.dot_general(a, b, (((1,), (0,)), ((), ())), preferred_element_type=F32)


def mmt(a, b):
    return lax.dot_general(a, b, (((1,), (1,)), ((), ())), preferred_element_type=F32)


def iota(shape, dim):
    return lax.broadcasted_iota(jnp.int32, shape, dim)


def one(cond):
    return jnp.where(cond, 1.0, 0.0).astype(BF16)


def host_bf16(cond):
    return np.asarray(cond, np.float32).astype(ml_dtypes.bfloat16)


def tile_constants():
    row, col = np.arange(128)[:, None], np.arange(128)[None, :]
    pick_x = host_bf16(col == 4 * (row % 32) + row // 32)
    r, c = np.arange(512)[:, None], np.arange(1024)[None, :]
    xi, quarter, z, y8 = r // 128, r // 32 % 4, r // 8 % 4, r % 8
    yt, j = c // 128, c % 64
    place = host_bf16(
        (2 * quarter + y8 // 4 == yt) & (z == j // 16) & (y8 % 4 == j // 4 % 4) & (xi == j % 4)
    )
    r, c = np.arange(64)[:, None], np.arange(128)[None, :]
    pick_j = host_bf16((c < 64) & (c % 4 == r // 16) & (c // 4 == r % 16))
    r, c = np.arange(512)[:, None], np.arange(512)[None, :]
    spread_x = host_bf16((r // 32 % 4 == c // 128) & (c % 128 == 4 * (r % 32) + r // 128))
    return pick_x, place, pick_j, spread_x


def weight_constants():
    lane = np.arange(384)
    band1 = np.zeros((2, 9, 6, 256), np.float32)
    fold1 = np.zeros((384, 1152), np.float32)
    for a in range(3):
        for b in range(3):
            for e in range(3):
                for c in range(2):
                    band1[c, 3 * a + b, 2 * e + c, (a * 3 + e) * 16 + b] = 1.0
                    fold1[
                        ((c * 3 + a) * 3 + e) * 16 + 3 + b, 128 * (3 * a + b) + 97 + 2 * e + c
                    ] = 1.0
    fold1[288, 103] = 1.0
    band3 = np.zeros((3, 9, 256), np.float32)
    for a in range(3):
        for b in range(3):
            for e in range(3):
                band3[e, 3 * (2 - a) + (2 - b), (a * 3 + e) * 16 + b] = 1.0
    rep3 = np.zeros((3, 96, 384), np.float32)
    for e in range(3):
        rep3[e, 32 * e + lane % 32, lane] = 1.0
    fold3 = np.zeros((3, 384, 128), np.float32)
    for e in range(3):
        live = lane[lane < 320]
        fold3[e, live, 32 * e + live % 32] = 1.0
    return tuple(host_bf16(x) for x in (band1, band3, rep3, fold1, fold3))


def own_order():
    return one(iota((64, 64), 1) == 2 * (iota((64, 64), 0) % 32) + iota((64, 64), 0) // 32)


def choose_tiles(pattern_ref, angle_ref, choice, chosen, first):
    order = own_order()
    lanes = iota((64, 256), 1)
    lines = []
    for g in range(VIEWS):
        held = pattern_ref[g].astype(F32).astype(BF16)
        ids = mmt(order, held).astype(jnp.int32)
        for k in range(16):
            at = 256 * k + 64 * g
            choice[at : at + 64, :] = one(lanes == ids[:, k : k + 1])
        lines.append(mmt(held, order))
    line = jnp.concatenate(lines, axis=1).astype(jnp.int32)
    tile = iota((128, 256), 0) + first
    for k in range(16):
        at = 128 * (k % 2)
        chosen[at : at + 128, 256 * (k // 2) : 256 * (k // 2) + 256] = one(
            tile == line[k : k + 1, :]
        )
    angles = mmt(order, angle_ref[...].astype(F32).astype(BF16)).astype(jnp.int32)
    return jnp.concatenate([angles[:, g : g + 1] for g in range(VIEWS)], axis=0)


def project(field_rows, choice, angles, response_ref, pick_x_ref, place_ref):
    by_x = mmt(pick_x_ref[...], field_rows).astype(BF16)
    wide = jnp.concatenate([by_x[32 * i : 32 * i + 32] for i in range(4)], axis=1)
    spread = mm(wide, place_ref[...]).astype(BF16)
    tiles = jnp.concatenate([spread[:, 128 * i : 128 * i + 128] for i in range(8)], axis=0)
    low = iota((256, 128), 1) < 64
    pairs = []
    for p in range(8):
        picked = mm(choice[512 * p : 512 * p + 512, :], tiles)
        pairs.append(jnp.where(low, picked[:256], picked[256:]).astype(BF16))
    lines = mmt(jnp.concatenate(pairs, axis=1), response_ref[...])
    half = iota((256, 128), 1) // 64
    total = jnp.zeros((256, 128), F32)
    for p in range(4):
        total = total + jnp.where(angles == 2 * p + half, lines[:, 128 * p : 128 * p + 128], 0.0)
    return total + pltpu.roll(total, 64, 1)


def doubled_rows(ref, part):
    low = iota((32, 128), 1) < 64
    parts = []
    for g in range(VIEWS):
        rows = ref[g, part]
        turned = pltpu.roll(rows, 64, 1)
        parts.append(jnp.where(low, rows, turned))
        parts.append(jnp.where(low, turned, rows))
    return jnp.concatenate(parts, axis=0)


def backproject(doubled, chosen, angles, response_ref, pick_j_ref, spread_x_ref, count):
    half = iota((256, 128), 1) // 64
    masked = [
        jnp.where(angles == 2 * p + half, doubled, 0.0).astype(BF16) for p in range(4)
    ]
    contrib = mm(jnp.concatenate(masked, axis=1), response_ref[...])
    high = contrib.astype(BF16)
    rest = (contrib - high.astype(F32)).astype(BF16)
    stacked = jnp.concatenate(
        [
            jnp.concatenate(
                [high[:, 128 * p : 128 * p + 128], rest[:, 128 * p : 128 * p + 128]], axis=1
            )
            for p in range(8)
        ],
        axis=0,
    )
    skip = (128 - count) // 2
    left = jnp.concatenate(
        [chosen[skip : skip + count, :], chosen[128 + skip : 128 + skip + count, :]], axis=0
    )
    sums = mm(left, stacked)
    sums = sums[:, :128] + sums[:, 128:]
    tiles = sums[:count] + pltpu.roll(sums[count:], 64, 1)
    top = tiles.astype(BF16)
    if count == 64:
        top = jnp.concatenate([top, (tiles - top.astype(F32)).astype(BF16)], axis=0)
    by_j = mmt(pick_j_ref[...], top).astype(BF16)
    wide = jnp.concatenate([by_j[16 * i : 16 * i + 16] for i in range(4)], axis=1)
    return mm(wide, spread_x_ref[...])


def start_copies(pairs, sems):
    copies = []
    for n, (source, target, device) in enumerate(pairs):
        copies.append(
            pltpu.make_async_remote_copy(
                src_ref=source,
                dst_ref=target,
                send_sem=sems.at[0, n],
                recv_sem=sems.at[1, n],
                device_id=device,
                device_id_type=MESH,
            )
        )
    for copy in copies:
        copy.start()
    return copies


def wait_in(copies):
    for copy in copies:
        copy.wait_recv()


def wait_out(copies):
    for copy in copies:
        copy.wait_send()


def shifted(value, e, lane):
    if e == 1:
        return value
    if e == 0:
        return jnp.where(lane == 0, 0.0, pltpu.roll(value, 1, 1))
    return jnp.where(lane == 127, 0.0, pltpu.roll(value, 127, 1))


def prepare_weights(
    w1_ref, w2_ref, w3_ref, band1_ref, band3_ref, rep3_ref, t1v, t1b, t3t, t3, t1t, w2r, w2t
):
    eye32 = one(iota((32, 32), 0) == iota((32, 32), 1))
    for c, ref in ((0, t1v), (1, t1b)):
        base = jnp.zeros((32, 256), F32)
        for tap in range(9):
            turned = mmt(eye32, w1_ref[tap]).astype(BF16)
            base = base + mm(turned, band1_ref[c, tap])
        for yo in range(12):
            ref[32 * yo : 32 * yo + 32, :] = pltpu.roll(base, yo + 1, 1).astype(BF16)
    eye96 = one(iota((96, 96), 0) == iota((96, 96), 1))
    w3 = w3_ref[...]
    w3_turned = mmt(eye96, w3).astype(BF16)
    base = jnp.zeros((32, 256), F32)
    for e in range(3):
        base = base + mm(w3_turned[32 * (2 - e) : 32 * (2 - e) + 32], band3_ref[e])
    for yo in range(10):
        t3t[32 * yo : 32 * yo + 32, :] = pltpu.roll(base, yo + 2, 1).astype(BF16)
    step = iota((8, 384), 1) // 32 - iota((8, 384), 0)
    for e in range(3):
        line = mm(w3, rep3_ref[e])
        for a in range(3):
            block = jnp.zeros((8, 384), F32)
            for b in range(3):
                block = block + jnp.where(step == b, line[3 * a + b : 3 * a + b + 1, :], 0.0)
            t3[8 * (3 * a + e) : 8 * (3 * a + e) + 8, :] = block
    rep = one(iota((32, 256), 0) == iota((32, 256), 1) % 32)
    turned = [mm(w1_ref[tap], rep) for tap in range(9)]
    row16 = iota((16, 256), 0)
    row_y = jnp.where(row16 < 8, row16, jnp.where(row16 == 8, -1, 8))
    step = iota((16, 256), 1) // 32 - row_y + 1
    step = jnp.where(row16 < 10, step, -1)
    for a in range(3):
        for c in range(2):
            for e in range(3):
                row = 2 * (2 - e) + c
                block = jnp.zeros((16, 256), F32)
                for b in range(3):
                    tap = 3 * (2 - a) + (2 - b)
                    block = block + jnp.where(step == b, turned[tap][row : row + 1, :], 0.0)
                at = 16 * ((a * 2 + c) * 3 + e)
                t1t[at : at + 16, :] = block.astype(BF16)
    places = [one(iota((96, 384), 1) == iota((96, 384), 0) + 96 * b) for b in range(3)]
    keep = iota((96, 96), 1) // 32 == 2 - iota((96, 96), 0) // 32
    same = one(iota((32, 96), 0) == iota((32, 96), 1) % 32)
    for a in range(3):
        plain = jnp.zeros((32, 384), F32)
        across = jnp.zeros((32, 384), F32)
        for b in range(3):
            plain = plain + mm(w2_ref[3 * a + b], places[b])
            tower = jnp.concatenate([w2_ref[3 * (2 - a) + (2 - b)].astype(F32)] * 3, axis=0)
            tower = jnp.where(keep, tower, 0.0).astype(BF16)
            across = across + mm(mmt(same, tower).astype(BF16), places[b])
        w2r[32 * a : 32 * a + 32, :] = plain.astype(BF16)
        w2t[32 * a : 32 * a + 32, :] = across.astype(BF16)


def pair_of(ref, z, count):
    cols = [jnp.concatenate([ref[z + n + a] for a in range(count)], axis=0) for n in range(2)]
    return jnp.concatenate(cols, axis=1)


def stacked_rows(ref, z, y):
    cols = [ref[z + n, pl.ds(y, 3)].reshape(288, 128) for n in range(2)]
    return jnp.concatenate(cols, axis=1)


def split_pairs(outs):
    return [out[:, 128 * n : 128 * n + 128] for out in outs for n in range(2)]


def step_kernel(
    volume_ref,
    upstream_ref,
    measured_ref,
    gain_ref,
    pattern_ref,
    angle_ref,
    w1_ref,
    bias1_ref,
    w2_ref,
    bias2_ref,
    w3_ref,
    pick_x_ref,
    pick_j_ref,
    band1_ref,
    band3_ref,
    response_hbm,
    place_hbm,
    spread_x_hbm,
    rep3_hbm,
    fold1_hbm,
    fold3_hbm,
    new_ref,
    grad_ref,
    total_ref,
    response_ref,
    place_ref,
    spread_x_ref,
    rep3_ref,
    fold1_ref,
    fold3_ref,
    slots,
    slots_low,
    slots_high,
    lines,
    choice,
    chosen,
    fields,
    ins,
    backs,
    ups,
    ups_own,
    t1v,
    t1b,
    t3t,
    t3,
    t1t,
    w2r,
    w2t,
    pre1,
    h3,
    ct3,
    h2,
    s3,
    s2z,
    s1,
    g2,
    g3,
    parts_own,
    parts,
    edges,
    edges_low,
    edges_high,
    sums,
    ring_in,
    view_in,
    layer_in,
    local_sems,
    volume_sems,
    line_sems,
    ups_sems,
    plane_sems,
    back_sems,
    part_sems,
    low_sems,
    high_sems,
    ring_sems,
    view_sems,
    layer_sems,
    final_sems,
):
    slab, member = lax.axis_index("slab"), lax.axis_index("view")
    above, below = lax.rem(slab + 1, SLABS), lax.rem(slab + SLABS - 1, SLABS)
    left, right = lax.rem(member + VIEWS - 1, VIEWS), lax.rem(member + 1, VIEWS)
    place, layer = lax.rem(slab, RING), lax.div(slab, RING)
    view_peers = [lax.rem(member + off, VIEWS) for off in range(1, VIEWS)]
    ring_peers = [layer * RING + lax.rem(place + off, RING) for off in range(1, RING)]
    layer_peers = [
        lax.rem(layer + off, LAYERS) * RING + place for off in range(1, LAYERS)
    ]
    depth, height = 4 * SLABS, 8 * VIEWS

    loads = [
        pltpu.make_async_copy(source, target, local_sems.at[n])
        for n, (source, target) in enumerate(
            (
                (place_hbm, place_ref),
                (response_hbm, response_ref),
                (rep3_hbm, rep3_ref),
                (spread_x_hbm, spread_x_ref),
                (fold1_hbm, fold1_ref),
                (fold3_hbm, fold3_ref),
            )
        )
    ]
    for load in loads:
        load.start()

    barrier = pltpu.get_barrier_semaphore()
    peers = [{"view": peer} for peer in view_peers]
    peers += [{"slab": peer} for peer in ring_peers + layer_peers]
    for off in range(VIEWS):
        view = lax.rem(member + off, VIEWS)
        peers += [{"slab": above, "view": view}, {"slab": below, "view": view}]
    for peer in peers:
        pl.semaphore_signal(barrier, inc=1, device_id=peer, device_id_type=MESH)
    slots[0, member] = volume_ref[...]
    slots[1, member] = upstream_ref[...].astype(F32)
    lines[member, 0] = measured_ref[...]
    lines[member, 1] = gain_ref[...]
    pl.semaphore_wait(barrier, len(peers))

    pending = []
    volume_copies = start_copies(
        [(slots.at[0, member], slots.at[0, member], {"view": p}) for p in view_peers],
        volume_sems,
    )
    line_copies = start_copies(
        [(lines.at[member], lines.at[member], {"view": p}) for p in view_peers], line_sems
    )
    ups_copies = start_copies(
        [(slots.at[1, member], slots.at[1, member], {"view": p}) for p in view_peers],
        ups_sems,
    )
    pending += volume_copies + line_copies + ups_copies

    angles = choose_tiles(pattern_ref, angle_ref, choice, chosen, 64 * member - 32)
    loads[2].wait()
    prepare_weights(
        w1_ref, w2_ref, w3_ref, band1_ref, band3_ref, rep3_ref, t1v, t1b, t3t, t3, t1t, w2r, w2t
    )
    wait_in(line_copies)
    measured_rows, gain_rows = doubled_rows(lines, 0), doubled_rows(lines, 1)
    loads[0].wait()
    loads[1].wait()
    loads[3].wait()
    wait_in(volume_copies)
    wait_in(ups_copies)
    plane_copies = start_copies(
        [
            (slots.at[:, :, pl.ds(1, 3)], slots_low, {"slab": above}),
            (slots.at[:, :, pl.ds(0, 3)], slots_high, {"slab": below}),
        ],
        plane_sems,
    )
    pending += plane_copies

    field_rows = slots[0].reshape(128, 128).astype(BF16)
    got = project(field_rows, choice, angles, response_ref, pick_x_ref, place_ref)
    dual = (gain_rows * (got - measured_rows)).astype(BF16).astype(F32)
    spread = backproject(dual, chosen, angles, response_ref, pick_j_ref, spread_x_ref, 128)
    for z in range(4):
        for yt in range(4):
            fields[2, 4 + z, 4 * yt : 4 * yt + 4, :] = spread[
                4 * z : 4 * z + 4, 128 * yt : 128 * yt + 128
            ]
    back_copies = start_copies(
        [
            (fields.at[2, pl.ds(5, 3)], fields.at[2, pl.ds(1, 3)], {"slab": above}),
            (fields.at[2, pl.ds(4, 3)], fields.at[2, pl.ds(8, 3)], {"slab": below}),
        ],
        back_sems,
    )
    pending += back_copies

    wait_in(plane_copies)
    low_z, low_y = 4 * slab - 4, 8 * member - 4
    lane16 = iota((16, 128), 1)
    global_y = iota((16, 128), 0) + low_y
    inside_y = (global_y >= 0) & (global_y < height)
    lane8 = iota((8, 128), 1)
    for field in range(2):
        for z in range(1, 11):
            if z < 4:
                source, at = slots_low, z - 1
            elif z < 8:
                source, at = slots, z - 4
            else:
                source, at = slots_high, z - 8
            fields[field, z, 4:12, :] = source[field, member, at]
            fields[field, z, 0:4, :] = source[field, left, at, 4:8, :]
            fields[field, z, 12:16, :] = source[field, right, at, 0:4, :]

    def shifts_of(field, target):
        def one_plane(z, carry):
            inside = inside_y & (z + low_z >= 0) & (z + low_z < depth)
            plane = jnp.where(inside, fields[field, z], 0.0)
            plane = plane.astype(BF16).astype(F32)
            for e in range(3):
                target[z, 16 * e : 16 * e + 16, :] = shifted(plane, e, lane16).astype(BF16)
            return carry

        lax.fori_loop(1, 11, one_plane, 0, unroll=2)

    shifts_of(0, ins)
    shifts_of(1, ups)
    ups_own[...] = jnp.zeros(ups_own.shape, F32)
    for z in range(4):
        plane = slots[1, member, z]
        for e in range(3):
            ups_own[2 + z, e] = shifted(plane, 2 - e, lane8)

    def third_turned(p, carry):
        z = 2 * p
        out = mm(t3t[:, :144], pair_of(ups, z + 2, 3))
        ct3[z] = out[:, :128]
        ct3[z + 1] = out[:, 128:]
        return carry

    lax.fori_loop(0, 3, third_turned, 0)
    eye32 = iota((32, 32), 0) == iota((32, 32), 1)
    bias1 = jnp.sum(jnp.where(eye32, bias1_ref[...], 0.0), axis=1, keepdims=True)
    bias2 = jnp.sum(jnp.where(eye32, bias2_ref[...], 0.0), axis=1, keepdims=True)
    bias1_rows = jnp.concatenate([jnp.broadcast_to(bias1, (32, 128))] * 12, axis=0)

    def first_volume(p, carry):
        z = 2 * p
        out = mm(t1v[:, :144], pair_of(ins, z + 1, 3))
        pre1[z] = out[:, :128] + bias1_rows
        pre1[z + 1] = out[:, 128:] + bias1_rows
        return carry

    lax.fori_loop(0, 4, first_volume, 0)
    s2z[...] = jnp.zeros(s2z.shape, BF16)
    g2[...] = jnp.zeros(g2.shape, F32)
    g3[...] = jnp.zeros(g3.shape, F32)

    wait_in(back_copies)
    shifts_of(2, backs)

    def first_back(p, carry):
        z = 2 * p
        out = mm(t1b[:, :144], pair_of(backs, z + 1, 3))
        pre1[z] += out[:, :128]
        pre1[z + 1] += out[:, 128:]
        return carry

    lax.fori_loop(0, 4, first_back, 0)

    lane384 = iota((384, 128), 1)
    row_y1 = iota((384, 128), 0) // 32 + low_y + 2
    inside1 = (row_y1 >= 0) & (row_y1 < height)

    def activate(z, keep_slope):
        value = pre1[z]
        gate = 0.5 * jnp.tanh(0.5 * value) + 0.5
        act = value * gate
        if keep_slope:
            pre1[z] = gate + act * (1.0 - gate)
        inside = inside1 & (z + low_z + 2 >= 0) & (z + low_z + 2 < depth)
        act = jnp.where(inside, act, 0.0)
        for e in range(3):
            h3[z, :, 32 * e : 32 * e + 32, :] = (
                shifted(act, e, lane384).astype(BF16).reshape(12, 32, 128)
            )

    def activate_outer(n, carry):
        activate(n + 4 * (n // 2), False)
        return carry

    def activate_inner(n, carry):
        activate(n + 2, True)
        return carry

    lax.fori_loop(0, 4, activate_outer, 0)
    lax.fori_loop(0, 4, activate_inner, 0)

    lane32 = iota((32, 128), 1)

    def second(y, carry):
        out = split_pairs([mm(w2r[:, :288], stacked_rows(h3, 2 * p, y)) for p in range(4)])
        ok_y = (y + low_y + 3 >= 0) & (y + low_y + 3 < height)
        at = pl.multiple_of(32 * y, 32)
        for z in range(6):
            value = out[z][:32] + out[z + 1][32:64] + out[z + 2][64:] + bias2
            gate = 0.5 * jnp.tanh(0.5 * value) + 0.5
            act = value * gate
            slope = gate + act * (1.0 - gate)
            ok = ok_y & (z + low_z + 3 >= 0) & (z + low_z + 3 < depth)
            live = jnp.where(ok, 1.0, 0.0)
            h2[z, pl.ds(at, 32), :] = (act * live).astype(BF16)
            slope = slope * ct3[z, pl.ds(at, 32), :] * live
            for e in range(3):
                s3[z, y, 32 * e : 32 * e + 32, :] = shifted(slope, e, lane32).astype(BF16)
        return carry

    lax.fori_loop(0, 10, second, 0)

    def second_turned(y, carry):
        out = split_pairs([mm(w2t[:, :288], stacked_rows(s3, 2 * p, y)) for p in range(3)])
        at = pl.multiple_of(32 * y, 32)
        from_ = pl.multiple_of(32 * y + 64, 32)
        for z in range(4):
            value = out[z][:32] + out[z + 1][32:64] + out[z + 2][64:]
            s1[z, pl.ds(at, 32), :] = (value * pre1[z + 2, pl.ds(from_, 32), :]).astype(BF16)
        return carry

    lax.fori_loop(0, 8, second_turned, 0)

    out = split_pairs([mm(t1t[...], pair_of(s1, 2 * p, 1)) for p in range(2)])
    for c in range(2):
        for z in range(-1, 5):
            total = jnp.zeros((16, 128), F32)
            for e in range(3):
                part = jnp.zeros((16, 128), F32)
                for a in range(3):
                    if 0 <= z + a - 1 < 4:
                        at = 16 * ((a * 2 + c) * 3 + e)
                        part = part + out[z + a - 1][at : at + 16]
                total = total + shifted(part, e, lane16)
            if z == -1:
                edges[0, c] = total.astype(BF16)
            elif z == 4:
                edges[1, c] = total.astype(BF16)
            else:
                parts[member, c, z] = total.astype(BF16)
                if c == 0:
                    parts_own[z] = total
    part_copies = start_copies(
        [(parts.at[member], parts.at[member], {"view": p}) for p in view_peers], part_sems
    )
    all_views = [lax.rem(member + off, VIEWS) for off in range(VIEWS)]
    low_copies = start_copies(
        [
            (edges.at[1], edges_low.at[member], {"slab": above, "view": view})
            for view in all_views
        ],
        low_sems,
    )
    high_copies = start_copies(
        [
            (edges.at[0], edges_high.at[member], {"slab": below, "view": view})
            for view in all_views
        ],
        high_sems,
    )
    pending += part_copies + low_copies + high_copies

    for z in range(4):
        s2z[z + 2] = s3[z + 1, 1:9, 32:64, :]
    ones = jnp.ones((16, 768), BF16)

    def second_grad(y, carry):
        turned = jnp.concatenate(
            [
                jnp.concatenate([s2z[z + 1 - a, y] for z in range(1, 7)], axis=1)
                for a in range(3)
            ],
            axis=0,
        )
        plain = jnp.concatenate(
            [h3[z, pl.ds(y + 1, 3)].reshape(288, 128) for z in range(1, 7)], axis=1
        )
        g2[:, :304] += mmt(turned, jnp.concatenate([plain, ones], axis=0))
        return carry

    lax.fori_loop(0, 8, second_grad, 0)

    turned = jnp.concatenate(
        [
            jnp.concatenate(
                [ups_own[z + 2 - a, e] for a in range(3) for e in range(3)], axis=0
            ).astype(BF16)
            for z in range(6)
        ],
        axis=1,
    )
    plain = jnp.concatenate([h2[z] for z in range(6)], axis=1)
    cross = mmt(turned, plain)
    step10 = iota((8, 320), 1) // 32 - iota((8, 320), 0)
    for a in range(3):
        for e in range(3):
            block = cross[8 * (3 * a + e) : 8 * (3 * a + e) + 8]
            for b in range(3):
                g3[e, 3 * a + b : 3 * a + b + 1, 0:320] = jnp.sum(
                    jnp.where(step10 == b, block, 0.0), axis=0, keepdims=True
                )
    loads[4].wait()
    loads[5].wait()
    third = jnp.zeros((16, 128), F32)
    for e in range(3):
        value = g3[e]
        high = value.astype(BF16)
        rest = (value - high.astype(F32)).astype(BF16)
        third = third + mm(high, fold3_ref[e]) + mm(rest, fold3_ref[e])

    turned = jnp.concatenate([s1[z] for z in range(4)], axis=1)
    plain = jnp.concatenate(
        [
            jnp.concatenate(
                [ins[z + 3 + a] for a in range(3)]
                + [backs[z + 3 + a] for a in range(3)]
                + [jnp.ones((96, 128), BF16)],
                axis=0,
            )
            for z in range(4)
        ],
        axis=1,
    )
    cross = mmt(turned, plain)
    total = cross[:32]
    for yo in range(1, 8):
        total = total + pltpu.roll(cross[32 * yo : 32 * yo + 32], 384 - yo, 1)
    high = total.astype(BF16)
    rest = (total - high.astype(F32)).astype(BF16)
    first_grads = mm(high, fold1_ref[...]) + mm(rest, fold1_ref[...])

    lanes = iota((32, 128), 1)
    for tap in range(9):
        a, b = tap // 3, tap % 3
        block = g2[32 * a : 32 * a + 32, :]
        if b:
            block = pltpu.roll(block, 384 - 96 * b, 1)
        block = jnp.where(lanes < (97 if b == 2 else 96), block[:, :128], 0.0)
        block = block + first_grads[:, 128 * tap : 128 * tap + 128]
        sums[4 * tap : 4 * tap + 4] = block.reshape(4, 8, 128)
    sums[36:38] = third.reshape(2, 8, 128)
    sums[38:40] = jnp.zeros((2, 8, 128), F32)

    ring_in[place] = sums[pl.ds(PIECE * place, PIECE)]
    ring_copies = start_copies(
        [
            (sums.at[pl.ds(PIECE * lax.rem(peer, RING), PIECE)], ring_in.at[place], {"slab": peer})
            for peer in ring_peers
        ],
        ring_sems,
    )
    pending += ring_copies

    t3_now = t3[:, :320].astype(BF16)
    out = split_pairs([mm(t3_now, pair_of(h2, 2 * p, 1)) for p in range(3)])
    for z in range(4):
        total = volume_ref[z]
        for e in range(3):
            part = jnp.zeros((8, 128), F32)
            for a in range(3):
                at = 8 * (3 * a + e)
                part = part + out[z + a][at : at + 8]
            total = total + shifted(part, e, lane8)
        new_ref[z] = total

    def add_up(ref, count):
        total = ref[0]
        for n in range(1, count):
            total = total + ref[n]
        return total

    wait_in(part_copies)
    wait_in(low_copies)
    wait_in(high_copies)
    has_low = jnp.where(slab > 0, 1.0, 0.0)
    has_high = jnp.where(slab < SLABS - 1, 1.0, 0.0)

    def plane_at(view, c, z):
        plane = parts[view, c, z].astype(F32)
        if z == 0:
            plane = plane + has_low * edges_low[view, c].astype(F32)
        if z == 3:
            plane = plane + has_high * edges_high[view, c].astype(F32)
        return plane

    row8 = iota((8, 128), 0)
    rows = [None] * 16
    for z in range(4):
        planes = [plane_at(view, 1, z) for view in range(VIEWS)]
        for view in range(VIEWS):
            value = planes[view][:8]
            if view > 0:
                value = value + jnp.where(row8 == 0, planes[view - 1][9:10], 0.0)
            if view < VIEWS - 1:
                value = value + jnp.where(row8 == 7, planes[view + 1][8:9], 0.0)
            rows[4 * view + z] = value
    field_rows = jnp.concatenate(rows, axis=0).astype(BF16)
    got = project(field_rows, choice, angles, response_ref, pick_x_ref, place_ref)
    wait_in(ring_copies)
    view_in[member] = add_up(ring_in, RING)
    view_copies = start_copies(
        [(view_in.at[member], view_in.at[member], {"view": p}) for p in view_peers], view_sems
    )
    echo = (gain_rows * got).astype(BF16).astype(F32)
    spread = backproject(echo, chosen, angles, response_ref, pick_j_ref, spread_x_ref, 64)
    spread = spread[:, :256] + spread[:, 256:]
    has_left = jnp.where(member > 0, 1.0, 0.0)
    has_right = jnp.where(member < VIEWS - 1, 1.0, 0.0)
    for z in range(4):
        value = parts_own[z]
        if z == 0:
            value = value + has_low * edges_low[member, 0].astype(F32)
        if z == 3:
            value = value + has_high * edges_high[member, 0].astype(F32)
        value = value[:8] + upstream_ref[z].astype(F32)
        value = value + jnp.where(row8 == 0, has_left * plane_at(left, 0, z)[9:10], 0.0)
        value = value + jnp.where(row8 == 7, has_right * plane_at(right, 0, z)[8:9], 0.0)
        for yt in range(2):
            grad_ref[z, 4 * yt : 4 * yt + 4, :] = (
                value[4 * yt : 4 * yt + 4, :]
                + spread[4 * z : 4 * z + 4, 128 * yt : 128 * yt + 128]
            )
    wait_in(view_copies)
    layer_in[layer] = add_up(view_in, VIEWS)
    layer_copies = start_copies(
        [(layer_in.at[layer], layer_in.at[layer], {"slab": p}) for p in layer_peers],
        layer_sems,
    )
    wait_out(pending)
    wait_in(layer_copies)
    mine = pl.ds(PIECE * place, PIECE)
    total_ref[mine] = add_up(layer_in, LAYERS)
    final_copies = start_copies(
        [(total_ref.at[mine], total_ref.at[mine], {"slab": p}) for p in ring_peers],
        final_sems,
    )
    wait_in(final_copies)
    wait_out(view_copies + layer_copies + final_copies)


def emit_kernel(
    scale,
    new_ref,
    grad_ref,
    total_ref,
    new_out,
    grad_out,
    w1_out,
    bias1_out,
    w2_out,
    bias2_out,
    w3_out,
):
    new_out[...] = new_ref[...]
    grad_out[...] = grad_ref[...]
    for tap in range(9):
        block = total_ref[4 * tap : 4 * tap + 4].reshape(32, 128) * scale
        w2_out[tap] = block[:, :96]
        turned = block.T
        w1_out[tap] = turned[97:103, :]
        if tap == 0:
            bias1_out[...] = turned[103:104, :]
        if tap == 5:
            bias2_out[...] = turned[96:97, :]
    third = total_ref[36:38].reshape(16, 128) * scale
    for tap in range(9):
        w3_out[tap] = third[tap : tap + 1, :96]


def vmem_specs(count):
    return [pl.BlockSpec(memory_space=pltpu.VMEM)] * count


def body(volume, measured, dual_gain, pattern, angle, response, w1, bias1, w2, bias2, w3, upstream):
    pick_x, place, pick_j, spread_x = [jnp.asarray(x) for x in tile_constants()]
    band1, band3, rep3, fold1, fold3 = [jnp.asarray(x) for x in weight_constants()]
    dma = pltpu.SemaphoreType.DMA
    pieces = PIECE * RING
    new_volume, grad_volume, total = pl.pallas_call(
        step_kernel,
        name="step",
        out_shape=(
            jax.ShapeDtypeStruct((4, 8, 128), F32),
            jax.ShapeDtypeStruct((4, 8, 128), F32),
            jax.ShapeDtypeStruct((pieces, 8, 128), F32),
        ),
        in_specs=vmem_specs(15) + [pl.BlockSpec(memory_space=HELD)] * 6,
        out_specs=tuple(vmem_specs(3)),
        scratch_shapes=[
            pltpu.VMEM((512, 1024), BF16),
            pltpu.VMEM((512, 1024), BF16),
            pltpu.VMEM((512, 512), BF16),
            pltpu.VMEM((3, 96, 384), BF16),
            pltpu.VMEM((384, 1152), BF16),
            pltpu.VMEM((3, 384, 128), BF16),
            pltpu.VMEM((2, VIEWS, 4, 8, 128), F32),
            pltpu.VMEM((2, VIEWS, 3, 8, 128), F32),
            pltpu.VMEM((2, VIEWS, 3, 8, 128), F32),
            pltpu.VMEM((VIEWS, 2, 32, 128), F32),
            pltpu.VMEM((4096, 256), BF16),
            pltpu.VMEM((256, 2048), BF16),
            pltpu.VMEM((3, 12, 16, 128), F32),
            pltpu.VMEM((12, 48, 128), BF16),
            pltpu.VMEM((12, 48, 128), BF16),
            pltpu.VMEM((12, 48, 128), BF16),
            pltpu.VMEM((8, 3, 8, 128), F32),
            pltpu.VMEM((384, 256), BF16),
            pltpu.VMEM((384, 256), BF16),
            pltpu.VMEM((320, 256), BF16),
            pltpu.VMEM((72, 384), F32),
            pltpu.VMEM((288, 256), BF16),
            pltpu.VMEM((96, 384), BF16),
            pltpu.VMEM((96, 384), BF16),
            pltpu.VMEM((8, 384, 128), F32),
            pltpu.VMEM((8, 12, 96, 128), BF16),
            pltpu.VMEM((6, 320, 128), F32),
            pltpu.VMEM((6, 320, 128), BF16),
            pltpu.VMEM((6, 10, 96, 128), BF16),
            pltpu.VMEM((8, 8, 32, 128), BF16),
            pltpu.VMEM((4, 256, 128), BF16),
            pltpu.VMEM((96, 384), F32),
            pltpu.VMEM((3, 16, 384), F32),
            pltpu.VMEM((4, 16, 128), F32),
            pltpu.VMEM((VIEWS, 2, 4, 16, 128), BF16),
            pltpu.VMEM((2, 2, 16, 128), BF16),
            pltpu.VMEM((VIEWS, 2, 16, 128), BF16),
            pltpu.VMEM((VIEWS, 2, 16, 128), BF16),
            pltpu.VMEM((pieces, 8, 128), F32),
            pltpu.VMEM((RING, PIECE, 8, 128), F32),
            pltpu.VMEM((VIEWS, PIECE, 8, 128), F32),
            pltpu.VMEM((LAYERS, PIECE, 8, 128), F32),
            dma((6,)),
            dma((2, 3)),
            dma((2, 3)),
            dma((2, 3)),
            dma((2, 2)),
            dma((2, 2)),
            dma((2, 3)),
            dma((2, 4)),
            dma((2, 4)),
            dma((2, RING - 1)),
            dma((2, 3)),
            dma((2, 3)),
            dma((2, RING - 1)),
        ],
        compiler_params=pltpu.CompilerParams(
            collective_id=0, has_side_effects=True, vmem_limit_bytes=VMEM_BYTES
        ),
    )(
        volume,
        upstream,
        measured.reshape(32, 128),
        dual_gain.reshape(32, 128),
        pattern.transpose(0, 1, 3, 2).reshape(VIEWS, 16, 64),
        angle.reshape(VIEWS, 64),
        w1.transpose(0, 2, 1),
        bias1.reshape(1, 32),
        w2,
        bias2.reshape(1, 32),
        w3.reshape(9, 96),
        pick_x,
        pick_j,
        band1,
        band3,
        response,
        place,
        spread_x,
        rep3,
        fold1,
        fold3,
    )
    scale = 1.0 / math.sqrt(volume.size * SLABS * VIEWS)
    new_volume, grad_volume, grad_w1, grad_bias1, grad_w2, grad_bias2, grad_w3 = pl.pallas_call(
        functools.partial(emit_kernel, scale),
        name="emit",
        out_shape=(
            jax.ShapeDtypeStruct((4, 8, 128), F32),
            jax.ShapeDtypeStruct((4, 8, 128), F32),
            jax.ShapeDtypeStruct((9, 6, 32), F32),
            jax.ShapeDtypeStruct((1, 32), F32),
            jax.ShapeDtypeStruct((9, 32, 96), F32),
            jax.ShapeDtypeStruct((1, 32), F32),
            jax.ShapeDtypeStruct((9, 1, 96), F32),
        ),
        in_specs=vmem_specs(3),
        out_specs=tuple(vmem_specs(7)),
    )(new_volume, grad_volume, total)
    return (
        new_volume,
        grad_volume,
        grad_w1.transpose(0, 2, 1),
        grad_bias1.reshape(32),
        grad_w2,
        grad_bias2.reshape(32),
        grad_w3,
    )


def solution(mesh):
    placed = (
        P("slab", "view", None),
        P("view", "slab", None),
        P("view", "slab", None),
        P(None, "slab", None, None),
        P(None, "slab", None),
        P(),
        P(),
        P(),
        P(),
        P(),
        P(),
        P("slab", "view", None),
    )
    return jax.shard_map(
        body,
        mesh=mesh,
        in_specs=placed,
        out_specs=(P("slab", "view", None), P("slab", "view", None), P(), P(), P(), P(), P()),
        check_vma=False,
    )
```

time: 533 us -> 55.5 us (0.10)
  the two profiles are of different devices: /device:TPU:31 before, /device:TPU:0 now
where the time goes in v2:
time: 55.5 us; the launch traced here: 55.3 us
  Pallas kernels  54.6 us (98%)
  between operations  0.65 us (1%)
    pallas_call x1, Pallas kernels, body(): pl.pallas_call(step_kernel, name='step', out_shape=(jax.ShapeDtypeStruct(...  52.9 us
    pallas_call x1, Pallas kernels, body(): pl.pallas_call(functools.partial(emit_kernel, scale), name='emit', out_sh...  1.79 us

profile of v2, /device:TPU:0, one launch (start us, length us, event | category | flops | bytes accessed | tf_op | source)
XLA Modules:
  0.0 55.3 jit_solution(5061910207262700608)
XLA Ops:
  0.6 52.9 %step.1 = (f32[4,8,128]{2,1,0:T(8,128)}, f32[4,8,128]{2,1,0:T(8,128)}, f32[40,8,128]{2,1,0:T(8,128)}) custom-call(f32[4,8,128]{2,1,0:T(8,128)} %volume_ref.1, bf16[4,8,128]{2,1,0:T(8,128)(2,1)} %upstream_ref.1, f32[32,128]{1,0:T(8,128)} %bitcast.17, f32[32,128]{1,0:T(8,128)} %bitcast.18, s32[4,16,64]{2,1,0:T(8,128)} %bitcast.15, s32[4,64]{1,0:T(4,128)} %bitcast.20, ...), custom_call_target="tpu_custom_call" | custom-call | tf_op jit(solution)/shard_map/step/pallas_call | solution.py:848
  53.5 1.8 %emit.1 = (f32[4,8,128]{2,1,0:T(8,128)}, f32[4,8,128]{2,1,0:T(8,128)}, f32[9,6,32]{2,1,0:T(8,128)}, f32[1,32]{1,0:T(1,128)}, f32[9,32,96]{2,1,0:T(8,128)}, /*index=5*/f32[1,32]{1,0:T(1,128)}, f32[9,1,96]{2,1,0:T(1,128)}) custom-call(f32[4,8,128]{2,1,0:T(8,128)} %get-tuple-element.17.new_ref, f32[4,8,128]{2,1,0:T(8,128)} %get-tuple-element.18.grad_ref, ...), custom_call_target="tpu_custom_call" | custom-call | tf_op jit(solution)/shard_map/emit/pallas_call | solution.py:942

commit v3 on v2

--- a/solution.py
+++ b/solution.py
@@ -17,7 +17,9 @@
 RING = 8
 LAYERS = 4
 SLABS = RING * LAYERS
-PIECE = 5
+PIECE = 40
+SMALL = 32
+MESSAGE = SMALL + PIECE
 VMEM_BYTES = 56 * 1024 * 1024
 HELD = pl.ANY
 
@@ -61,16 +63,16 @@
 def weight_constants():
     lane = np.arange(384)
     band1 = np.zeros((2, 9, 6, 256), np.float32)
-    fold1 = np.zeros((384, 1152), np.float32)
+    fold1 = np.zeros((384, 128), np.float32)
     for a in range(3):
         for b in range(3):
             for e in range(3):
                 for c in range(2):
                     band1[c, 3 * a + b, 2 * e + c, (a * 3 + e) * 16 + b] = 1.0
                     fold1[
-                        ((c * 3 + a) * 3 + e) * 16 + 3 + b, 128 * (3 * a + b) + 97 + 2 * e + c
+                        ((c * 3 + a) * 3 + e) * 16 + 3 + b, 6 * (3 * a + b) + 2 * e + c
                     ] = 1.0
-    fold1[288, 103] = 1.0
+    fold1[288, 54] = 1.0
     band3 = np.zeros((3, 9, 256), np.float32)
     for a in range(3):
         for b in range(3):
@@ -134,7 +136,7 @@
     low = iota((32, 128), 1) < 64
     parts = []
     for g in range(VIEWS):
-        rows = ref[g, part]
+        rows = ref[g, part].astype(F32)
         turned = pltpu.roll(rows, 64, 1)
         parts.append(jnp.where(low, rows, turned))
         parts.append(jnp.where(low, turned, rows))
@@ -305,17 +307,16 @@
     fold3_hbm,
     new_ref,
     grad_ref,
-    total_ref,
+    final_in,
     response_ref,
     place_ref,
     spread_x_ref,
     rep3_ref,
     fold1_ref,
     fold3_ref,
-    slots,
-    slots_low,
-    slots_high,
-    lines,
+    pack,
+    pack_low,
+    pack_high,
     choice,
     chosen,
     fields,
@@ -341,22 +342,22 @@
     g3,
     parts_own,
     parts,
+    parts_side,
     edges,
     edges_low,
     edges_high,
+    totals,
     sums,
     ring_in,
     view_in,
     layer_in,
     local_sems,
-    volume_sems,
-    line_sems,
-    ups_sems,
+    pack_sems,
     plane_sems,
     back_sems,
+    edge_sems,
     part_sems,
-    low_sems,
-    high_sems,
+    side_sems,
     ring_sems,
     view_sems,
     layer_sems,
@@ -391,56 +392,42 @@
 
     barrier = pltpu.get_barrier_semaphore()
     peers = [{"view": peer} for peer in view_peers]
-    peers += [{"slab": peer} for peer in ring_peers + layer_peers]
-    for off in range(VIEWS):
-        view = lax.rem(member + off, VIEWS)
-        peers += [{"slab": above, "view": view}, {"slab": below, "view": view}]
+    peers += [{"slab": peer} for peer in ring_peers + layer_peers + [above, below]]
     for peer in peers:
         pl.semaphore_signal(barrier, inc=1, device_id=peer, device_id_type=MESH)
-    slots[0, member] = volume_ref[...]
-    slots[1, member] = upstream_ref[...].astype(F32)
-    lines[member, 0] = measured_ref[...]
-    lines[member, 1] = gain_ref[...]
+    pack[member, 0] = volume_ref[...].reshape(32, 128).astype(BF16)
+    pack[member, 1] = upstream_ref[...].astype(F32).reshape(32, 128).astype(BF16)
+    pack[member, 2] = measured_ref[...].astype(BF16)
+    pack[member, 3] = gain_ref[...].astype(BF16)
     pl.semaphore_wait(barrier, len(peers))
 
     pending = []
-    volume_copies = start_copies(
-        [(slots.at[0, member], slots.at[0, member], {"view": p}) for p in view_peers],
-        volume_sems,
-    )
-    line_copies = start_copies(
-        [(lines.at[member], lines.at[member], {"view": p}) for p in view_peers], line_sems
-    )
-    ups_copies = start_copies(
-        [(slots.at[1, member], slots.at[1, member], {"view": p}) for p in view_peers],
-        ups_sems,
-    )
-    pending += volume_copies + line_copies + ups_copies
-
+    pack_copies = start_copies(
+        [(pack.at[member], pack.at[member], {"view": p}) for p in view_peers], pack_sems
+    )
+    pending += pack_copies
     angles = choose_tiles(pattern_ref, angle_ref, choice, chosen, 64 * member - 32)
     loads[2].wait()
     prepare_weights(
         w1_ref, w2_ref, w3_ref, band1_ref, band3_ref, rep3_ref, t1v, t1b, t3t, t3, t1t, w2r, w2t
     )
-    wait_in(line_copies)
-    measured_rows, gain_rows = doubled_rows(lines, 0), doubled_rows(lines, 1)
     loads[0].wait()
     loads[1].wait()
     loads[3].wait()
-    wait_in(volume_copies)
-    wait_in(ups_copies)
+    wait_in(pack_copies)
     plane_copies = start_copies(
         [
-            (slots.at[:, :, pl.ds(1, 3)], slots_low, {"slab": above}),
-            (slots.at[:, :, pl.ds(0, 3)], slots_high, {"slab": below}),
+            (pack.at[:, pl.ds(0, 2)], pack_low, {"slab": above}),
+            (pack.at[:, pl.ds(0, 2)], pack_high, {"slab": below}),
         ],
         plane_sems,
     )
     pending += plane_copies
 
-    field_rows = slots[0].reshape(128, 128).astype(BF16)
+    field_rows = pack[:, 0].reshape(128, 128)
     got = project(field_rows, choice, angles, response_ref, pick_x_ref, place_ref)
-    dual = (gain_rows * (got - measured_rows)).astype(BF16).astype(F32)
+    gain_rows = doubled_rows(pack, 3)
+    dual = (gain_rows * (got - doubled_rows(pack, 2))).astype(BF16).astype(F32)
     spread = backproject(dual, chosen, angles, response_ref, pick_j_ref, spread_x_ref, 128)
     for z in range(4):
         for yt in range(4):
@@ -463,16 +450,15 @@
     inside_y = (global_y >= 0) & (global_y < height)
     lane8 = iota((8, 128), 1)
     for field in range(2):
-        for z in range(1, 11):
-            if z < 4:
-                source, at = slots_low, z - 1
-            elif z < 8:
-                source, at = slots, z - 4
-            else:
-                source, at = slots_high, z - 8
-            fields[field, z, 4:12, :] = source[field, member, at]
-            fields[field, z, 0:4, :] = source[field, left, at, 4:8, :]
-            fields[field, z, 12:16, :] = source[field, right, at, 0:4, :]
+        for source, first, low in ((pack_low, 1, 0), (pack, 4, 4), (pack_high, 8, 8)):
+            own, before, after = (
+                source[view, field].astype(F32) for view in (member, left, right)
+            )
+            for z in range(first, min(low + 4, 11)):
+                at = 8 * (z - low)
+                fields[field, z, 4:12, :] = own[at : at + 8]
+                fields[field, z, 0:4, :] = before[at + 4 : at + 8]
+                fields[field, z, 12:16, :] = after[at : at + 4]
 
     def shifts_of(field, target):
         def one_plane(z, carry):
@@ -489,7 +475,7 @@
     shifts_of(1, ups)
     ups_own[...] = jnp.zeros(ups_own.shape, F32)
     for z in range(4):
-        plane = slots[1, member, z]
+        plane = upstream_ref[z].astype(F32)
         for e in range(3):
             ups_own[2 + z, e] = shifted(plane, 2 - e, lane8)
 
@@ -578,56 +564,6 @@
         return carry
 
     lax.fori_loop(0, 10, second, 0)
-
-    def second_turned(y, carry):
-        out = split_pairs([mm(w2t[:, :288], stacked_rows(s3, 2 * p, y)) for p in range(3)])
-        at = pl.multiple_of(32 * y, 32)
-        from_ = pl.multiple_of(32 * y + 64, 32)
-        for z in range(4):
-            value = out[z][:32] + out[z + 1][32:64] + out[z + 2][64:]
-            s1[z, pl.ds(at, 32), :] = (value * pre1[z + 2, pl.ds(from_, 32), :]).astype(BF16)
-        return carry
-
-    lax.fori_loop(0, 8, second_turned, 0)
-
-    out = split_pairs([mm(t1t[...], pair_of(s1, 2 * p, 1)) for p in range(2)])
-    for c in range(2):
-        for z in range(-1, 5):
-            total = jnp.zeros((16, 128), F32)
-            for e in range(3):
-                part = jnp.zeros((16, 128), F32)
-                for a in range(3):
-                    if 0 <= z + a - 1 < 4:
-                        at = 16 * ((a * 2 + c) * 3 + e)
-                        part = part + out[z + a - 1][at : at + 16]
-                total = total + shifted(part, e, lane16)
-            if z == -1:
-                edges[0, c] = total.astype(BF16)
-            elif z == 4:
-                edges[1, c] = total.astype(BF16)
-            else:
-                parts[member, c, z] = total.astype(BF16)
-                if c == 0:
-                    parts_own[z] = total
-    part_copies = start_copies(
-        [(parts.at[member], parts.at[member], {"view": p}) for p in view_peers], part_sems
-    )
-    all_views = [lax.rem(member + off, VIEWS) for off in range(VIEWS)]
-    low_copies = start_copies(
-        [
-            (edges.at[1], edges_low.at[member], {"slab": above, "view": view})
-            for view in all_views
-        ],
-        low_sems,
-    )
-    high_copies = start_copies(
-        [
-            (edges.at[0], edges_high.at[member], {"slab": below, "view": view})
-            for view in all_views
-        ],
-        high_sems,
-    )
-    pending += part_copies + low_copies + high_copies
 
     for z in range(4):
         s2z[z + 2] = s3[z + 1, 1:9, 32:64, :]
@@ -677,6 +613,63 @@
         rest = (value - high.astype(F32)).astype(BF16)
         third = third + mm(high, fold3_ref[e]) + mm(rest, fold3_ref[e])
 
+    lanes = iota((32, 128), 1)
+    for tap in range(9):
+        a, b = tap // 3, tap % 3
+        block = g2[32 * a : 32 * a + 32, :]
+        if b:
+            block = pltpu.roll(block, 384 - 96 * b, 1)
+        totals[32 * tap : 32 * tap + 32, :] = jnp.where(
+            lanes < (97 if b == 2 else 96), block[:, :128], 0.0
+        )
+    totals[288:304, :] = third
+    totals[304:320, :] = jnp.zeros((16, 128), F32)
+    for n in range(RING):
+        sums[n] = totals[PIECE * n : PIECE * n + PIECE, :].astype(BF16)
+    ring_in[place] = sums[place]
+    ring_copies = start_copies(
+        [(sums.at[lax.rem(peer, RING)], ring_in.at[place], {"slab": peer}) for peer in ring_peers],
+        ring_sems,
+    )
+    pending += ring_copies
+
+    def second_turned(y, carry):
+        out = split_pairs([mm(w2t[:, :288], stacked_rows(s3, 2 * p, y)) for p in range(3)])
+        at = pl.multiple_of(32 * y, 32)
+        from_ = pl.multiple_of(32 * y + 64, 32)
+        for z in range(4):
+            value = out[z][:32] + out[z + 1][32:64] + out[z + 2][64:]
+            s1[z, pl.ds(at, 32), :] = (value * pre1[z + 2, pl.ds(from_, 32), :]).astype(BF16)
+        return carry
+
+    lax.fori_loop(0, 8, second_turned, 0)
+
+    out = split_pairs([mm(t1t[...], pair_of(s1, 2 * p, 1)) for p in range(2)])
+    for c in range(2):
+        for z in range(-1, 5):
+            total = jnp.zeros((16, 128), F32)
+            for e in range(3):
+                part = jnp.zeros((16, 128), F32)
+                for a in range(3):
+                    if 0 <= z + a - 1 < 4:
+                        at = 16 * ((a * 2 + c) * 3 + e)
+                        part = part + out[z + a - 1][at : at + 16]
+                total = total + shifted(part, e, lane16)
+            if z == -1:
+                edges[0, c] = total.astype(BF16)
+            elif z == 4:
+                edges[1, c] = total.astype(BF16)
+            else:
+                parts_own[c, z] = total
+    edge_copies = start_copies(
+        [
+            (edges.at[1], edges_low, {"slab": above}),
+            (edges.at[0], edges_high, {"slab": below}),
+        ],
+        edge_sems,
+    )
+    pending += edge_copies
+
     turned = jnp.concatenate([s1[z] for z in range(4)], axis=1)
     plain = jnp.concatenate(
         [
@@ -696,29 +689,32 @@
         total = total + pltpu.roll(cross[32 * yo : 32 * yo + 32], 384 - yo, 1)
     high = total.astype(BF16)
     rest = (total - high.astype(F32)).astype(BF16)
-    first_grads = mm(high, fold1_ref[...]) + mm(rest, fold1_ref[...])
-
-    lanes = iota((32, 128), 1)
-    for tap in range(9):
-        a, b = tap // 3, tap % 3
-        block = g2[32 * a : 32 * a + 32, :]
-        if b:
-            block = pltpu.roll(block, 384 - 96 * b, 1)
-        block = jnp.where(lanes < (97 if b == 2 else 96), block[:, :128], 0.0)
-        block = block + first_grads[:, 128 * tap : 128 * tap + 128]
-        sums[4 * tap : 4 * tap + 4] = block.reshape(4, 8, 128)
-    sums[36:38] = third.reshape(2, 8, 128)
-    sums[38:40] = jnp.zeros((2, 8, 128), F32)
-
-    ring_in[place] = sums[pl.ds(PIECE * place, PIECE)]
-    ring_copies = start_copies(
-        [
-            (sums.at[pl.ds(PIECE * lax.rem(peer, RING), PIECE)], ring_in.at[place], {"slab": peer})
-            for peer in ring_peers
-        ],
-        ring_sems,
-    )
-    pending += ring_copies
+    view_in[member, 0:SMALL, :] = (mm(high, fold1_ref[...]) + mm(rest, fold1_ref[...])).astype(BF16)
+
+    wait_in(ring_copies)
+    ring_total = ring_in[0].astype(F32)
+    for n in range(1, RING):
+        ring_total = ring_total + ring_in[n].astype(F32)
+    view_in[member, SMALL:, :] = ring_total.astype(BF16)
+    view_copies = start_copies(
+        [(view_in.at[member], view_in.at[member], {"view": p}) for p in view_peers], view_sems
+    )
+
+    wait_in(edge_copies)
+    has_low = jnp.where(slab > 0, 1.0, 0.0)
+    has_high = jnp.where(slab < SLABS - 1, 1.0, 0.0)
+    for c in (1, 0):
+        parts_own[c, 0] += has_low * edges_low[c].astype(F32)
+        parts_own[c, 3] += has_high * edges_high[c].astype(F32)
+        (parts if c else parts_side)[member] = parts_own[c].astype(BF16)
+    part_copies = start_copies(
+        [(parts.at[member], parts.at[member], {"view": p}) for p in view_peers], part_sems
+    )
+    side_copies = start_copies(
+        [(parts_side.at[member], parts_side.at[member], {"view": p}) for p in view_peers],
+        side_sems,
+    )
+    pending += part_copies + side_copies
 
     t3_now = t3[:, :320].astype(BF16)
     out = split_pairs([mm(t3_now, pair_of(h2, 2 * p, 1)) for p in range(3)])
@@ -732,30 +728,24 @@
             total = total + shifted(part, e, lane8)
         new_ref[z] = total
 
-    def add_up(ref, count):
-        total = ref[0]
-        for n in range(1, count):
-            total = total + ref[n]
-        return total
+    def sum_views():
+        total = view_in[0].astype(F32)
+        for n in range(1, VIEWS):
+            total = total + view_in[n].astype(F32)
+        return total.astype(BF16)
+
+    wait_in(view_copies)
+    layer_in[layer] = sum_views()
+    layer_copies = start_copies(
+        [(layer_in.at[layer], layer_in.at[layer], {"slab": p}) for p in layer_peers],
+        layer_sems,
+    )
 
     wait_in(part_copies)
-    wait_in(low_copies)
-    wait_in(high_copies)
-    has_low = jnp.where(slab > 0, 1.0, 0.0)
-    has_high = jnp.where(slab < SLABS - 1, 1.0, 0.0)
-
-    def plane_at(view, c, z):
-        plane = parts[view, c, z].astype(F32)
-        if z == 0:
-            plane = plane + has_low * edges_low[view, c].astype(F32)
-        if z == 3:
-            plane = plane + has_high * edges_high[view, c].astype(F32)
-        return plane
-
     row8 = iota((8, 128), 0)
     rows = [None] * 16
     for z in range(4):
-        planes = [plane_at(view, 1, z) for view in range(VIEWS)]
+        planes = [parts[view, z].astype(F32) for view in range(VIEWS)]
         for view in range(VIEWS):
             value = planes[view][:8]
             if view > 0:
@@ -765,44 +755,32 @@
             rows[4 * view + z] = value
     field_rows = jnp.concatenate(rows, axis=0).astype(BF16)
     got = project(field_rows, choice, angles, response_ref, pick_x_ref, place_ref)
-    wait_in(ring_copies)
-    view_in[member] = add_up(ring_in, RING)
-    view_copies = start_copies(
-        [(view_in.at[member], view_in.at[member], {"view": p}) for p in view_peers], view_sems
+    wait_in(layer_copies)
+    layer_total = layer_in[0].astype(F32)
+    for n in range(1, LAYERS):
+        layer_total = layer_total + layer_in[n].astype(F32)
+    final_in[place] = layer_total.astype(BF16)
+    final_copies = start_copies(
+        [(final_in.at[place], final_in.at[place], {"slab": p}) for p in ring_peers],
+        final_sems,
     )
     echo = (gain_rows * got).astype(BF16).astype(F32)
     spread = backproject(echo, chosen, angles, response_ref, pick_j_ref, spread_x_ref, 64)
     spread = spread[:, :256] + spread[:, 256:]
+    wait_in(side_copies)
     has_left = jnp.where(member > 0, 1.0, 0.0)
     has_right = jnp.where(member < VIEWS - 1, 1.0, 0.0)
     for z in range(4):
-        value = parts_own[z]
-        if z == 0:
-            value = value + has_low * edges_low[member, 0].astype(F32)
-        if z == 3:
-            value = value + has_high * edges_high[member, 0].astype(F32)
-        value = value[:8] + upstream_ref[z].astype(F32)
-        value = value + jnp.where(row8 == 0, has_left * plane_at(left, 0, z)[9:10], 0.0)
-        value = value + jnp.where(row8 == 7, has_right * plane_at(right, 0, z)[8:9], 0.0)
+        value = parts_own[0, z][:8] + upstream_ref[z].astype(F32)
+        before = has_left * parts_side[left, z].astype(F32)[9:10]
+        after = has_right * parts_side[right, z].astype(F32)[8:9]
+        value = value + jnp.where(row8 == 0, before, 0.0) + jnp.where(row8 == 7, after, 0.0)
         for yt in range(2):
             grad_ref[z, 4 * yt : 4 * yt + 4, :] = (
                 value[4 * yt : 4 * yt + 4, :]
                 + spread[4 * z : 4 * z + 4, 128 * yt : 128 * yt + 128]
             )
-    wait_in(view_copies)
-    layer_in[layer] = add_up(view_in, VIEWS)
-    layer_copies = start_copies(
-        [(layer_in.at[layer], layer_in.at[layer], {"slab": p}) for p in layer_peers],
-        layer_sems,
-    )
     wait_out(pending)
-    wait_in(layer_copies)
-    mine = pl.ds(PIECE * place, PIECE)
-    total_ref[mine] = add_up(layer_in, LAYERS)
-    final_copies = start_copies(
-        [(total_ref.at[mine], total_ref.at[mine], {"slab": p}) for p in ring_peers],
-        final_sems,
-    )
     wait_in(final_copies)
     wait_out(view_copies + layer_copies + final_copies)
 
@@ -822,18 +800,20 @@
 ):
     new_out[...] = new_ref[...]
     grad_out[...] = grad_ref[...]
+    whole = jnp.concatenate(
+        [total_ref[n, SMALL:, :].astype(F32) for n in range(RING)], axis=0
+    ) * scale
+    small = total_ref[0, :SMALL, :].astype(F32)
+    for n in range(1, RING):
+        small = small + total_ref[n, :SMALL, :].astype(F32)
+    turned = (small * scale).T
+    bias1_out[...] = turned[54:55, :]
     for tap in range(9):
-        block = total_ref[4 * tap : 4 * tap + 4].reshape(32, 128) * scale
+        block = whole[32 * tap : 32 * tap + 32]
         w2_out[tap] = block[:, :96]
-        turned = block.T
-        w1_out[tap] = turned[97:103, :]
-        if tap == 0:
-            bias1_out[...] = turned[103:104, :]
-        if tap == 5:
-            bias2_out[...] = turned[96:97, :]
-    third = total_ref[36:38].reshape(16, 128) * scale
-    for tap in range(9):
-        w3_out[tap] = third[tap : tap + 1, :96]
+        w1_out[tap] = turned[6 * tap : 6 * tap + 6, :]
+        w3_out[tap] = whole[288 + tap : 289 + tap, :96]
+    bias2_out[...] = whole[160:192].T[96:97, :]
 
 
 def vmem_specs(count):
@@ -844,14 +824,13 @@
     pick_x, place, pick_j, spread_x = [jnp.asarray(x) for x in tile_constants()]
     band1, band3, rep3, fold1, fold3 = [jnp.asarray(x) for x in weight_constants()]
     dma = pltpu.SemaphoreType.DMA
-    pieces = PIECE * RING
     new_volume, grad_volume, total = pl.pallas_call(
         step_kernel,
         name="step",
         out_shape=(
             jax.ShapeDtypeStruct((4, 8, 128), F32),
             jax.ShapeDtypeStruct((4, 8, 128), F32),
-            jax.ShapeDtypeStruct((pieces, 8, 128), F32),
+            jax.ShapeDtypeStruct((RING, MESSAGE, 128), BF16),
         ),
         in_specs=vmem_specs(15) + [pl.BlockSpec(memory_space=HELD)] * 6,
         out_specs=tuple(vmem_specs(3)),
@@ -860,12 +839,11 @@
             pltpu.VMEM((512, 1024), BF16),
             pltpu.VMEM((512, 512), BF16),
             pltpu.VMEM((3, 96, 384), BF16),
-            pltpu.VMEM((384, 1152), BF16),
+            pltpu.VMEM((384, 128), BF16),
             pltpu.VMEM((3, 384, 128), BF16),
-            pltpu.VMEM((2, VIEWS, 4, 8, 128), F32),
-            pltpu.VMEM((2, VIEWS, 3, 8, 128), F32),
-            pltpu.VMEM((2, VIEWS, 3, 8, 128), F32),
-            pltpu.VMEM((VIEWS, 2, 32, 128), F32),
+            pltpu.VMEM((VIEWS, 4, 32, 128), BF16),
+            pltpu.VMEM((VIEWS, 2, 32, 128), BF16),
+            pltpu.VMEM((VIEWS, 2, 32, 128), BF16),
             pltpu.VMEM((4096, 256), BF16),
             pltpu.VMEM((256, 2048), BF16),
             pltpu.VMEM((3, 12, 16, 128), F32),
@@ -889,24 +867,24 @@
             pltpu.VMEM((4, 256, 128), BF16),
             pltpu.VMEM((96, 384), F32),
             pltpu.VMEM((3, 16, 384), F32),
-            pltpu.VMEM((4, 16, 128), F32),
-            pltpu.VMEM((VIEWS, 2, 4, 16, 128), BF16),
+            pltpu.VMEM((2, 4, 16, 128), F32),
+            pltpu.VMEM((VIEWS, 4, 16, 128), BF16),
+            pltpu.VMEM((VIEWS, 4, 16, 128), BF16),
             pltpu.VMEM((2, 2, 16, 128), BF16),
-            pltpu.VMEM((VIEWS, 2, 16, 128), BF16),
-            pltpu.VMEM((VIEWS, 2, 16, 128), BF16),
-            pltpu.VMEM((pieces, 8, 128), F32),
-            pltpu.VMEM((RING, PIECE, 8, 128), F32),
-            pltpu.VMEM((VIEWS, PIECE, 8, 128), F32),
-            pltpu.VMEM((LAYERS, PIECE, 8, 128), F32),
+            pltpu.VMEM((2, 16, 128), BF16),
+            pltpu.VMEM((2, 16, 128), BF16),
+            pltpu.VMEM((RING * PIECE, 128), F32),
+            pltpu.VMEM((RING, PIECE, 128), BF16),
+            pltpu.VMEM((RING, PIECE, 128), BF16),
+            pltpu.VMEM((VIEWS, MESSAGE, 128), BF16),
+            pltpu.VMEM((LAYERS, MESSAGE, 128), BF16),
             dma((6,)),
-            dma((2, 3)),
-            dma((2, 3)),
             dma((2, 3)),
             dma((2, 2)),
             dma((2, 2)),
+            dma((2, 2)),
             dma((2, 3)),
-            dma((2, 4)),
-            dma((2, 4)),
+            dma((2, 3)),
             dma((2, RING - 1)),
             dma((2, 3)),
             dma((2, 3)),

time: 55.5 us -> 48.8 us (0.88); the launches traced: 55.3 us -> 48 us
  Pallas kernels: 54.6 us -> 47.4 us
    pallas_call x1, Pallas kernels: 52.9 us -> 45.7 us  [body(): pl.pallas_call(step_kernel, name='step', out_shape=(jax.ShapeDtypeStruct(...]
where the time goes in v3:
time: 48.8 us; the launch traced here: 48 us
  Pallas kernels  47.4 us (97%)
  between operations  0.65 us (1%)
    pallas_call x1, Pallas kernels, body(): pl.pallas_call(step_kernel, name='step', out_shape=(jax.ShapeDtypeStruct(...  45.7 us
    pallas_call x1, Pallas kernels, body(): pl.pallas_call(functools.partial(emit_kernel, scale), name='emit', out_sh...  1.72 us

profile of v3, /device:TPU:0, one launch (start us, length us, event | category | flops | bytes accessed | tf_op | source)
XLA Modules:
  0.0 48.0 jit_solution(720477650056219532)
XLA Ops:
  0.6 45.7 %step.1 = (f32[4,8,128]{2,1,0:T(8,128)}, f32[4,8,128]{2,1,0:T(8,128)}, bf16[8,72,128]{2,1,0:T(8,128)(2,1)}) custom-call(f32[4,8,128]{2,1,0:T(8,128)} %volume_ref.1, bf16[4,8,128]{2,1,0:T(8,128)(2,1)} %upstream_ref.1, f32[32,128]{1,0:T(8,128)} %bitcast.17, f32[32,128]{1,0:T(8,128)} %bitcast.18, s32[4,16,64]{2,1,0:T(8,128)} %bitcast.15, s32[4,64]{1,0:T(4,128)} %bitcast.20, ...), custom_call_target="tpu_custom_call" | custom-call | tf_op jit(solution)/shard_map/step/pallas_call | solution.py:827
  46.3 1.7 %emit.1 = (f32[4,8,128]{2,1,0:T(8,128)}, f32[4,8,128]{2,1,0:T(8,128)}, f32[9,6,32]{2,1,0:T(8,128)}, f32[1,32]{1,0:T(1,128)}, f32[9,32,96]{2,1,0:T(8,128)}, /*index=5*/f32[1,32]{1,0:T(1,128)}, f32[9,1,96]{2,1,0:T(1,128)}) custom-call(f32[4,8,128]{2,1,0:T(8,128)} %get-tuple-element.17.new_ref, f32[4,8,128]{2,1,0:T(8,128)} %get-tuple-element.18.grad_ref, ...), custom_call_target="tpu_custom_call" | custom-call | tf_op jit(solution)/shard_map/emit/pallas_call | solution.py:920

commit v4 on v3

--- a/solution.py
+++ b/solution.py
@@ -284,6 +284,30 @@
 
 
 def step_kernel(
+    volume_hbm,
+    upstream_hbm,
+    measured_hbm,
+    gain_hbm,
+    pattern_hbm,
+    angle_hbm,
+    w1_hbm,
+    bias1_hbm,
+    w2_hbm,
+    bias2_hbm,
+    w3_hbm,
+    pick_x_hbm,
+    pick_j_hbm,
+    band1_hbm,
+    band3_hbm,
+    response_hbm,
+    place_hbm,
+    spread_x_hbm,
+    rep3_hbm,
+    fold1_hbm,
+    fold3_hbm,
+    new_ref,
+    grad_ref,
+    final_in,
     volume_ref,
     upstream_ref,
     measured_ref,
@@ -299,15 +323,6 @@
     pick_j_ref,
     band1_ref,
     band3_ref,
-    response_hbm,
-    place_hbm,
-    spread_x_hbm,
-    rep3_hbm,
-    fold1_hbm,
-    fold3_hbm,
-    new_ref,
-    grad_ref,
-    final_in,
     response_ref,
     place_ref,
     spread_x_ref,
@@ -367,34 +382,57 @@
     above, below = lax.rem(slab + 1, SLABS), lax.rem(slab + SLABS - 1, SLABS)
     left, right = lax.rem(member + VIEWS - 1, VIEWS), lax.rem(member + 1, VIEWS)
     place, layer = lax.rem(slab, RING), lax.div(slab, RING)
-    view_peers = [lax.rem(member + off, VIEWS) for off in range(1, VIEWS)]
+    view_peers = [
+        VIEWS - 1 - member,
+        lax.rem(member + 2, VIEWS),
+        member + 1 - 2 * lax.rem(member, 2),
+    ]
     ring_peers = [layer * RING + lax.rem(place + off, RING) for off in range(1, RING)]
     layer_peers = [
         lax.rem(layer + off, LAYERS) * RING + place for off in range(1, LAYERS)
     ]
     depth, height = 4 * SLABS, 8 * VIEWS
 
-    loads = [
-        pltpu.make_async_copy(source, target, local_sems.at[n])
-        for n, (source, target) in enumerate(
-            (
-                (place_hbm, place_ref),
-                (response_hbm, response_ref),
-                (rep3_hbm, rep3_ref),
-                (spread_x_hbm, spread_x_ref),
-                (fold1_hbm, fold1_ref),
-                (fold3_hbm, fold3_ref),
-            )
-        )
-    ]
-    for load in loads:
-        load.start()
-
     barrier = pltpu.get_barrier_semaphore()
     peers = [{"view": peer} for peer in view_peers]
     peers += [{"slab": peer} for peer in ring_peers + layer_peers + [above, below]]
     for peer in peers:
         pl.semaphore_signal(barrier, inc=1, device_id=peer, device_id_type=MESH)
+
+    loads = {}
+    for n, (name, source, target) in enumerate(
+        (
+            ("volume", volume_hbm, volume_ref),
+            ("upstream", upstream_hbm, upstream_ref),
+            ("measured", measured_hbm, measured_ref),
+            ("gain", gain_hbm, gain_ref),
+            ("pattern", pattern_hbm, pattern_ref),
+            ("angle", angle_hbm, angle_ref),
+            ("w1", w1_hbm, w1_ref),
+            ("w2", w2_hbm, w2_ref),
+            ("w3", w3_hbm, w3_ref),
+            ("band1", band1_hbm, band1_ref),
+            ("band3", band3_hbm, band3_ref),
+            ("rep3", rep3_hbm, rep3_ref),
+            ("pick_x", pick_x_hbm, pick_x_ref),
+            ("place", place_hbm, place_ref),
+            ("response", response_hbm, response_ref),
+            ("pick_j", pick_j_hbm, pick_j_ref),
+            ("spread_x", spread_x_hbm, spread_x_ref),
+            ("bias1", bias1_hbm, bias1_ref),
+            ("bias2", bias2_hbm, bias2_ref),
+            ("fold3", fold3_hbm, fold3_ref),
+            ("fold1", fold1_hbm, fold1_ref),
+        )
+    ):
+        loads[name] = pltpu.make_async_copy(source, target, local_sems.at[n])
+        loads[name].start()
+
+    def loaded(*which):
+        for name in which:
+            loads[name].wait()
+
+    loaded("volume", "upstream", "measured", "gain")
     pack[member, 0] = volume_ref[...].reshape(32, 128).astype(BF16)
     pack[member, 1] = upstream_ref[...].astype(F32).reshape(32, 128).astype(BF16)
     pack[member, 2] = measured_ref[...].astype(BF16)
@@ -406,14 +444,13 @@
         [(pack.at[member], pack.at[member], {"view": p}) for p in view_peers], pack_sems
     )
     pending += pack_copies
+    loaded("pattern", "angle")
     angles = choose_tiles(pattern_ref, angle_ref, choice, chosen, 64 * member - 32)
-    loads[2].wait()
+    loaded("w1", "w2", "w3", "band1", "band3", "rep3")
     prepare_weights(
         w1_ref, w2_ref, w3_ref, band1_ref, band3_ref, rep3_ref, t1v, t1b, t3t, t3, t1t, w2r, w2t
     )
-    loads[0].wait()
-    loads[1].wait()
-    loads[3].wait()
+    loaded("pick_x", "place", "response", "pick_j", "spread_x", "bias1", "bias2")
     wait_in(pack_copies)
     plane_copies = start_copies(
         [
@@ -469,7 +506,7 @@
                 target[z, 16 * e : 16 * e + 16, :] = shifted(plane, e, lane16).astype(BF16)
             return carry
 
-        lax.fori_loop(1, 11, one_plane, 0, unroll=2)
+        lax.fori_loop(1, 11, one_plane, 0, unroll=10)
 
     shifts_of(0, ins)
     shifts_of(1, ups)
@@ -486,7 +523,7 @@
         ct3[z + 1] = out[:, 128:]
         return carry
 
-    lax.fori_loop(0, 3, third_turned, 0)
+    lax.fori_loop(0, 3, third_turned, 0, unroll=3)
     eye32 = iota((32, 32), 0) == iota((32, 32), 1)
     bias1 = jnp.sum(jnp.where(eye32, bias1_ref[...], 0.0), axis=1, keepdims=True)
     bias2 = jnp.sum(jnp.where(eye32, bias2_ref[...], 0.0), axis=1, keepdims=True)
@@ -499,7 +536,7 @@
         pre1[z + 1] = out[:, 128:] + bias1_rows
         return carry
 
-    lax.fori_loop(0, 4, first_volume, 0)
+    lax.fori_loop(0, 4, first_volume, 0, unroll=4)
     s2z[...] = jnp.zeros(s2z.shape, BF16)
     g2[...] = jnp.zeros(g2.shape, F32)
     g3[...] = jnp.zeros(g3.shape, F32)
@@ -514,7 +551,7 @@
         pre1[z + 1] += out[:, 128:]
         return carry
 
-    lax.fori_loop(0, 4, first_back, 0)
+    lax.fori_loop(0, 4, first_back, 0, unroll=4)
 
     lane384 = iota((384, 128), 1)
     row_y1 = iota((384, 128), 0) // 32 + low_y + 2
@@ -541,8 +578,8 @@
         activate(n + 2, True)
         return carry
 
-    lax.fori_loop(0, 4, activate_outer, 0)
-    lax.fori_loop(0, 4, activate_inner, 0)
+    lax.fori_loop(0, 4, activate_outer, 0, unroll=4)
+    lax.fori_loop(0, 4, activate_inner, 0, unroll=4)
 
     lane32 = iota((32, 128), 1)
 
@@ -563,7 +600,7 @@
                 s3[z, y, 32 * e : 32 * e + 32, :] = shifted(slope, e, lane32).astype(BF16)
         return carry
 
-    lax.fori_loop(0, 10, second, 0)
+    lax.fori_loop(0, 10, second, 0, unroll=10)
 
     for z in range(4):
         s2z[z + 2] = s3[z + 1, 1:9, 32:64, :]
@@ -583,7 +620,7 @@
         g2[:, :304] += mmt(turned, jnp.concatenate([plain, ones], axis=0))
         return carry
 
-    lax.fori_loop(0, 8, second_grad, 0)
+    lax.fori_loop(0, 8, second_grad, 0, unroll=8)
 
     turned = jnp.concatenate(
         [
@@ -604,8 +641,7 @@
                 g3[e, 3 * a + b : 3 * a + b + 1, 0:320] = jnp.sum(
                     jnp.where(step10 == b, block, 0.0), axis=0, keepdims=True
                 )
-    loads[4].wait()
-    loads[5].wait()
+    loaded("fold1", "fold3")
     third = jnp.zeros((16, 128), F32)
     for e in range(3):
         value = g3[e]
@@ -642,7 +678,7 @@
             s1[z, pl.ds(at, 32), :] = (value * pre1[z + 2, pl.ds(from_, 32), :]).astype(BF16)
         return carry
 
-    lax.fori_loop(0, 8, second_turned, 0)
+    lax.fori_loop(0, 8, second_turned, 0, unroll=8)
 
     out = split_pairs([mm(t1t[...], pair_of(s1, 2 * p, 1)) for p in range(2)])
     for c in range(2):
@@ -832,9 +868,24 @@
             jax.ShapeDtypeStruct((4, 8, 128), F32),
             jax.ShapeDtypeStruct((RING, MESSAGE, 128), BF16),
         ),
-        in_specs=vmem_specs(15) + [pl.BlockSpec(memory_space=HELD)] * 6,
+        in_specs=[pl.BlockSpec(memory_space=HELD)] * 21,
         out_specs=tuple(vmem_specs(3)),
         scratch_shapes=[
+            pltpu.VMEM((4, 8, 128), F32),
+            pltpu.VMEM((4, 8, 128), BF16),
+            pltpu.VMEM((32, 128), F32),
+            pltpu.VMEM((32, 128), F32),
+            pltpu.VMEM((VIEWS, 16, 64), jnp.int32),
+            pltpu.VMEM((VIEWS, 64), jnp.int32),
+            pltpu.VMEM((9, 6, 32), BF16),
+            pltpu.VMEM((1, 32), F32),
+            pltpu.VMEM((9, 32, 96), BF16),
+            pltpu.VMEM((1, 32), F32),
+            pltpu.VMEM((9, 96), BF16),
+            pltpu.VMEM((128, 128), BF16),
+            pltpu.VMEM((64, 128), BF16),
+            pltpu.VMEM((2, 9, 6, 256), BF16),
+            pltpu.VMEM((3, 9, 256), BF16),
             pltpu.VMEM((512, 1024), BF16),
             pltpu.VMEM((512, 1024), BF16),
             pltpu.VMEM((512, 512), BF16),
@@ -878,7 +929,7 @@
             pltpu.VMEM((RING, PIECE, 128), BF16),
             pltpu.VMEM((VIEWS, MESSAGE, 128), BF16),
             pltpu.VMEM((LAYERS, MESSAGE, 128), BF16),
-            dma((6,)),
+            dma((21,)),
             dma((2, 3)),
             dma((2, 2)),
             dma((2, 2)),

time: 48.8 us -> 42.3 us (0.87); the launches traced: 48 us -> 42.1 us
  Pallas kernels: 47.4 us -> 41.5 us
    pallas_call x1, Pallas kernels: 45.7 us -> 39.8 us  [body(): pl.pallas_call(step_kernel, name='step', out_shape=(jax.ShapeDtypeStruct(...]
where the time goes in v4:
time: 42.3 us; the launch traced here: 42.1 us
  Pallas kernels  41.5 us (98%)
  between operations  0.65 us (2%)
    pallas_call x1, Pallas kernels, body(): pl.pallas_call(step_kernel, name='step', out_shape=(jax.ShapeDtypeStruct(...  39.8 us
    pallas_call x1, Pallas kernels, body(): pl.pallas_call(functools.partial(emit_kernel, scale), name='emit', out_sh...  1.72 us

profile of v4, /device:TPU:0, one launch (start us, length us, event | category | flops | bytes accessed | tf_op | source)
XLA Modules:
  0.0 42.1 jit_solution(4752722552677762565)
XLA Ops:
  0.6 39.8 %step.1 = (f32[4,8,128]{2,1,0:T(8,128)}, f32[4,8,128]{2,1,0:T(8,128)}, bf16[8,72,128]{2,1,0:T(8,128)(2,1)}) custom-call(f32[4,8,128]{2,1,0:T(8,128)} %volume_hbm.1, bf16[4,8,128]{2,1,0:T(8,128)(2,1)} %upstream_hbm.1, f32[32,128]{1,0:T(8,128)} %bitcast.17, f32[32,128]{1,0:T(8,128)} %bitcast.18, s32[4,16,64]{2,1,0:T(8,128)} %bitcast.15, s32[4,64]{1,0:T(4,128)} %bitcast.20, ...), custom_call_target="tpu_custom_call" | custom-call | tf_op jit(solution)/shard_map/step/pallas_call | solution.py:863
  40.4 1.7 %emit.1 = (f32[4,8,128]{2,1,0:T(8,128)}, f32[4,8,128]{2,1,0:T(8,128)}, f32[9,6,32]{2,1,0:T(8,128)}, f32[1,32]{1,0:T(1,128)}, f32[9,32,96]{2,1,0:T(8,128)}, /*index=5*/f32[1,32]{1,0:T(1,128)}, f32[9,1,96]{2,1,0:T(1,128)}) custom-call(f32[4,8,128]{2,1,0:T(8,128)} %get-tuple-element.17.new_ref, f32[4,8,128]{2,1,0:T(8,128)} %get-tuple-element.18.grad_ref, ...), custom_call_target="tpu_custom_call" | custom-call | tf_op jit(solution)/shard_map/emit/pallas_call | solution.py:971

commit v5 on v4

--- a/solution.py
+++ b/solution.py
@@ -18,7 +18,7 @@
 LAYERS = 4
 SLABS = RING * LAYERS
 PIECE = 40
-SMALL = 32
+SMALL = 16
 MESSAGE = SMALL + PIECE
 VMEM_BYTES = 56 * 1024 * 1024
 HELD = pl.ANY
@@ -100,8 +100,9 @@
         held = pattern_ref[g].astype(F32).astype(BF16)
         ids = mmt(order, held).astype(jnp.int32)
         for k in range(16):
-            at = 256 * k + 64 * g
-            choice[at : at + 64, :] = one(lanes == ids[:, k : k + 1])
+            at = 256 * (k // 2) + 64 * g
+            side = 256 * (k % 2)
+            choice[at : at + 64, side : side + 256] = one(lanes == ids[:, k : k + 1])
         lines.append(mmt(held, order))
     line = jnp.concatenate(lines, axis=1).astype(jnp.int32)
     tile = iota((128, 256), 0) + first
@@ -114,17 +115,19 @@
     return jnp.concatenate([angles[:, g : g + 1] for g in range(VIEWS)], axis=0)
 
 
-def project(field_rows, choice, angles, response_ref, pick_x_ref, place_ref):
+def project(field_rows, choice, angles, response_turned, pick_x_ref, place_ref):
     by_x = mmt(pick_x_ref[...], field_rows).astype(BF16)
     wide = jnp.concatenate([by_x[32 * i : 32 * i + 32] for i in range(4)], axis=1)
     spread = mm(wide, place_ref[...]).astype(BF16)
     tiles = jnp.concatenate([spread[:, 128 * i : 128 * i + 128] for i in range(8)], axis=0)
+    zero = jnp.zeros((256, 128), F32)
+    wide_tiles = tiles.astype(F32)
     low = iota((256, 128), 1) < 64
-    pairs = []
-    for p in range(8):
-        picked = mm(choice[512 * p : 512 * p + 512, :], tiles)
-        pairs.append(jnp.where(low, picked[:256], picked[256:]).astype(BF16))
-    lines = mmt(jnp.concatenate(pairs, axis=1), response_ref[...])
+    both = jnp.concatenate(
+        [jnp.where(low, wide_tiles, zero), jnp.where(low, zero, wide_tiles)], axis=0
+    ).astype(BF16)
+    pairs = [mm(choice[256 * p : 256 * p + 256, :], both).astype(BF16) for p in range(8)]
+    lines = mm(jnp.concatenate(pairs, axis=1), response_turned[...])
     half = iota((256, 128), 1) // 64
     total = jnp.zeros((256, 128), F32)
     for p in range(4):
@@ -150,22 +153,21 @@
     ]
     contrib = mm(jnp.concatenate(masked, axis=1), response_ref[...])
     high = contrib.astype(BF16)
-    rest = (contrib - high.astype(F32)).astype(BF16)
-    stacked = jnp.concatenate(
-        [
-            jnp.concatenate(
-                [high[:, 128 * p : 128 * p + 128], rest[:, 128 * p : 128 * p + 128]], axis=1
-            )
-            for p in range(8)
-        ],
-        axis=0,
-    )
+    blocks = [high[:, 128 * p : 128 * p + 128] for p in range(8)]
+    if count == 64:
+        rest = (contrib - high.astype(F32)).astype(BF16)
+        blocks = [
+            jnp.concatenate([block, rest[:, 128 * p : 128 * p + 128]], axis=1)
+            for p, block in enumerate(blocks)
+        ]
+    stacked = jnp.concatenate(blocks, axis=0)
     skip = (128 - count) // 2
     left = jnp.concatenate(
         [chosen[skip : skip + count, :], chosen[128 + skip : 128 + skip + count, :]], axis=0
     )
     sums = mm(left, stacked)
-    sums = sums[:, :128] + sums[:, 128:]
+    if count == 64:
+        sums = sums[:, :128] + sums[:, 128:]
     tiles = sums[:count] + pltpu.roll(sums[count:], 64, 1)
     top = tiles.astype(BF16)
     if count == 64:
@@ -357,7 +359,8 @@
     g3,
     parts_own,
     parts,
-    parts_side,
+    edge_rows,
+    response_turned,
     edges,
     edges_low,
     edges_high,
@@ -372,7 +375,6 @@
     back_sems,
     edge_sems,
     part_sems,
-    side_sems,
     ring_sems,
     view_sems,
     layer_sems,
@@ -451,6 +453,7 @@
         w1_ref, w2_ref, w3_ref, band1_ref, band3_ref, rep3_ref, t1v, t1b, t3t, t3, t1t, w2r, w2t
     )
     loaded("pick_x", "place", "response", "pick_j", "spread_x", "bias1", "bias2")
+    response_turned[...] = response_ref[...].T
     wait_in(pack_copies)
     plane_copies = start_copies(
         [
@@ -462,7 +465,7 @@
     pending += plane_copies
 
     field_rows = pack[:, 0].reshape(128, 128)
-    got = project(field_rows, choice, angles, response_ref, pick_x_ref, place_ref)
+    got = project(field_rows, choice, angles, response_turned, pick_x_ref, place_ref)
     gain_rows = doubled_rows(pack, 3)
     dual = (gain_rows * (got - doubled_rows(pack, 2))).astype(BF16).astype(F32)
     spread = backproject(dual, chosen, angles, response_ref, pick_j_ref, spread_x_ref, 128)
@@ -725,7 +728,10 @@
         total = total + pltpu.roll(cross[32 * yo : 32 * yo + 32], 384 - yo, 1)
     high = total.astype(BF16)
     rest = (total - high.astype(F32)).astype(BF16)
-    view_in[member, 0:SMALL, :] = (mm(high, fold1_ref[...]) + mm(rest, fold1_ref[...])).astype(BF16)
+    first_grads = mm(high, fold1_ref[...]) + mm(rest, fold1_ref[...])
+    view_in[member, 0:SMALL, :] = jnp.where(
+        iota((16, 128), 1) < 64, first_grads[:16], pltpu.roll(first_grads[16:], 64, 1)
+    ).astype(BF16)
 
     wait_in(ring_copies)
     ring_total = ring_in[0].astype(F32)
@@ -742,15 +748,17 @@
     for c in (1, 0):
         parts_own[c, 0] += has_low * edges_low[c].astype(F32)
         parts_own[c, 3] += has_high * edges_high[c].astype(F32)
-        (parts if c else parts_side)[member] = parts_own[c].astype(BF16)
+        for z in range(4):
+            at = 8 * (1 - c) + 2 * z
+            edge_rows[at : at + 2, :] = parts_own[c, z, 8:10, :]
+    parts[member, 0:32, :] = jnp.concatenate(
+        [parts_own[1, z, 0:8, :] for z in range(4)], axis=0
+    ).astype(BF16)
+    parts[member, 32:48, :] = edge_rows[...].astype(BF16)
     part_copies = start_copies(
         [(parts.at[member], parts.at[member], {"view": p}) for p in view_peers], part_sems
     )
-    side_copies = start_copies(
-        [(parts_side.at[member], parts_side.at[member], {"view": p}) for p in view_peers],
-        side_sems,
-    )
-    pending += part_copies + side_copies
+    pending += part_copies
 
     t3_now = t3[:, :320].astype(BF16)
     out = split_pairs([mm(t3_now, pair_of(h2, 2 * p, 1)) for p in range(3)])
@@ -780,17 +788,19 @@
     wait_in(part_copies)
     row8 = iota((8, 128), 0)
     rows = [None] * 16
+    planes = [parts[view].astype(F32) for view in range(VIEWS)]
     for z in range(4):
-        planes = [parts[view, z].astype(F32) for view in range(VIEWS)]
         for view in range(VIEWS):
-            value = planes[view][:8]
+            value = planes[view][8 * z : 8 * z + 8]
             if view > 0:
-                value = value + jnp.where(row8 == 0, planes[view - 1][9:10], 0.0)
+                edge = planes[view - 1][33 + 2 * z : 34 + 2 * z]
+                value = value + jnp.where(row8 == 0, edge, 0.0)
             if view < VIEWS - 1:
-                value = value + jnp.where(row8 == 7, planes[view + 1][8:9], 0.0)
+                edge = planes[view + 1][32 + 2 * z : 33 + 2 * z]
+                value = value + jnp.where(row8 == 7, edge, 0.0)
             rows[4 * view + z] = value
     field_rows = jnp.concatenate(rows, axis=0).astype(BF16)
-    got = project(field_rows, choice, angles, response_ref, pick_x_ref, place_ref)
+    got = project(field_rows, choice, angles, response_turned, pick_x_ref, place_ref)
     wait_in(layer_copies)
     layer_total = layer_in[0].astype(F32)
     for n in range(1, LAYERS):
@@ -803,14 +813,14 @@
     echo = (gain_rows * got).astype(BF16).astype(F32)
     spread = backproject(echo, chosen, angles, response_ref, pick_j_ref, spread_x_ref, 64)
     spread = spread[:, :256] + spread[:, 256:]
-    wait_in(side_copies)
     has_left = jnp.where(member > 0, 1.0, 0.0)
     has_right = jnp.where(member < VIEWS - 1, 1.0, 0.0)
+    before = has_left * parts[left, 32:48, :].astype(F32)
+    after = has_right * parts[right, 32:48, :].astype(F32)
     for z in range(4):
         value = parts_own[0, z][:8] + upstream_ref[z].astype(F32)
-        before = has_left * parts_side[left, z].astype(F32)[9:10]
-        after = has_right * parts_side[right, z].astype(F32)[8:9]
-        value = value + jnp.where(row8 == 0, before, 0.0) + jnp.where(row8 == 7, after, 0.0)
+        value = value + jnp.where(row8 == 0, before[9 + 2 * z : 10 + 2 * z], 0.0)
+        value = value + jnp.where(row8 == 7, after[8 + 2 * z : 9 + 2 * z], 0.0)
         for yt in range(2):
             grad_ref[z, 4 * yt : 4 * yt + 4, :] = (
                 value[4 * yt : 4 * yt + 4, :]
@@ -842,6 +852,7 @@
     small = total_ref[0, :SMALL, :].astype(F32)
     for n in range(1, RING):
         small = small + total_ref[n, :SMALL, :].astype(F32)
+    small = jnp.concatenate([small, pltpu.roll(small, 64, 1)], axis=0)
     turned = (small * scale).T
     bias1_out[...] = turned[54:55, :]
     for tap in range(9):
@@ -895,7 +906,7 @@
             pltpu.VMEM((VIEWS, 4, 32, 128), BF16),
             pltpu.VMEM((VIEWS, 2, 32, 128), BF16),
             pltpu.VMEM((VIEWS, 2, 32, 128), BF16),
-            pltpu.VMEM((4096, 256), BF16),
+            pltpu.VMEM((2048, 512), BF16),
             pltpu.VMEM((256, 2048), BF16),
             pltpu.VMEM((3, 12, 16, 128), F32),
             pltpu.VMEM((12, 48, 128), BF16),
@@ -919,8 +930,9 @@
             pltpu.VMEM((96, 384), F32),
             pltpu.VMEM((3, 16, 384), F32),
             pltpu.VMEM((2, 4, 16, 128), F32),
-            pltpu.VMEM((VIEWS, 4, 16, 128), BF16),
-            pltpu.VMEM((VIEWS, 4, 16, 128), BF16),
+            pltpu.VMEM((VIEWS, 48, 128), BF16),
+            pltpu.VMEM((16, 128), F32),
+            pltpu.VMEM((1024, 512), BF16),
             pltpu.VMEM((2, 2, 16, 128), BF16),
             pltpu.VMEM((2, 16, 128), BF16),
             pltpu.VMEM((2, 16, 128), BF16),
@@ -934,7 +946,6 @@
             dma((2, 2)),
             dma((2, 2)),
             dma((2, 2)),
-            dma((2, 3)),
             dma((2, 3)),
             dma((2, RING - 1)),
             dma((2, 3)),

time: 42.3 us -> 41.5 us (0.981)
  Pallas kernels: 41.5 us -> 40.7 us
    pallas_call x1, Pallas kernels: 39.8 us -> 39 us  [body(): pl.pallas_call(step_kernel, name='step', out_shape=(jax.ShapeDtypeStruct(...]
where the time goes in v5:
time: 41.5 us; the launch traced here: 41.4 us
  Pallas kernels  40.7 us (98%)
  between operations  0.65 us (2%)
    pallas_call x1, Pallas kernels, body(): pl.pallas_call(step_kernel, name='step', out_shape=(jax.ShapeDtypeStruct(...  39 us
    pallas_call x1, Pallas kernels, body(): pl.pallas_call(functools.partial(emit_kernel, scale), name='emit', out_sh...  1.77 us

profile of v5, /device:TPU:0, one launch (start us, length us, event | category | flops | bytes accessed | tf_op | source)
XLA Modules:
  0.0 41.4 jit_solution(10742116854445478782)
XLA Ops:
  0.6 39.0 %step.1 = (f32[4,8,128]{2,1,0:T(8,128)}, f32[4,8,128]{2,1,0:T(8,128)}, bf16[8,56,128]{2,1,0:T(8,128)(2,1)}) custom-call(f32[4,8,128]{2,1,0:T(8,128)} %volume_hbm.1, bf16[4,8,128]{2,1,0:T(8,128)(2,1)} %upstream_hbm.1, f32[32,128]{1,0:T(8,128)} %bitcast.17, f32[32,128]{1,0:T(8,128)} %bitcast.18, s32[4,16,64]{2,1,0:T(8,128)} %bitcast.15, s32[4,64]{1,0:T(4,128)} %bitcast.20, ...), custom_call_target="tpu_custom_call" | custom-call | tf_op jit(solution)/shard_map/step/pallas_call | solution.py:874
  39.6 1.8 %emit.1 = (f32[4,8,128]{2,1,0:T(8,128)}, f32[4,8,128]{2,1,0:T(8,128)}, f32[9,6,32]{2,1,0:T(8,128)}, f32[1,32]{1,0:T(1,128)}, f32[9,32,96]{2,1,0:T(8,128)}, /*index=5*/f32[1,32]{1,0:T(1,128)}, f32[9,1,96]{2,1,0:T(1,128)}) custom-call(f32[4,8,128]{2,1,0:T(8,128)} %get-tuple-element.17.new_ref, f32[4,8,128]{2,1,0:T(8,128)} %get-tuple-element.18.grad_ref, ...), custom_call_target="tpu_custom_call" | custom-call | tf_op jit(solution)/shard_map/emit/pallas_call | solution.py:982

commit v6 on v5

--- a/solution.py
+++ b/solution.py
@@ -337,6 +337,7 @@
     choice,
     chosen,
     fields,
+    back_planes,
     ins,
     backs,
     ups,
@@ -470,14 +471,12 @@
     dual = (gain_rows * (got - doubled_rows(pack, 2))).astype(BF16).astype(F32)
     spread = backproject(dual, chosen, angles, response_ref, pick_j_ref, spread_x_ref, 128)
     for z in range(4):
-        for yt in range(4):
-            fields[2, 4 + z, 4 * yt : 4 * yt + 4, :] = spread[
-                4 * z : 4 * z + 4, 128 * yt : 128 * yt + 128
-            ]
+        plane = [spread[4 * z : 4 * z + 4, 128 * yt : 128 * yt + 128] for yt in range(4)]
+        back_planes[4 + z] = jnp.concatenate(plane, axis=0).astype(BF16)
     back_copies = start_copies(
         [
-            (fields.at[2, pl.ds(5, 3)], fields.at[2, pl.ds(1, 3)], {"slab": above}),
-            (fields.at[2, pl.ds(4, 3)], fields.at[2, pl.ds(8, 3)], {"slab": below}),
+            (back_planes.at[pl.ds(5, 3)], back_planes.at[pl.ds(1, 3)], {"slab": above}),
+            (back_planes.at[pl.ds(4, 3)], back_planes.at[pl.ds(8, 3)], {"slab": below}),
         ],
         back_sems,
     )
@@ -503,7 +502,8 @@
     def shifts_of(field, target):
         def one_plane(z, carry):
             inside = inside_y & (z + low_z >= 0) & (z + low_z < depth)
-            plane = jnp.where(inside, fields[field, z], 0.0)
+            held = back_planes[z].astype(F32) if field == 2 else fields[field, z]
+            plane = jnp.where(inside, held, 0.0)
             plane = plane.astype(BF16).astype(F32)
             for e in range(3):
                 target[z, 16 * e : 16 * e + 16, :] = shifted(plane, e, lane16).astype(BF16)
@@ -908,7 +908,8 @@
             pltpu.VMEM((VIEWS, 2, 32, 128), BF16),
             pltpu.VMEM((2048, 512), BF16),
             pltpu.VMEM((256, 2048), BF16),
-            pltpu.VMEM((3, 12, 16, 128), F32),
+            pltpu.VMEM((2, 12, 16, 128), F32),
+            pltpu.VMEM((12, 16, 128), BF16),
             pltpu.VMEM((12, 48, 128), BF16),
             pltpu.VMEM((12, 48, 128), BF16),
             pltpu.VMEM((12, 48, 128), BF16),

time: 41.5 us -> 41.4 us (level)
  no operation moved by 1% of the time
where the time goes in v6:
time: 41.4 us; the launch traced here: 41.3 us
  Pallas kernels  40.6 us (98%)
  between operations  0.65 us (2%)
    pallas_call x1, Pallas kernels, body(): pl.pallas_call(step_kernel, name='step', out_shape=(jax.ShapeDtypeStruct(...  38.9 us
    pallas_call x1, Pallas kernels, body(): pl.pallas_call(functools.partial(emit_kernel, scale), name='emit', out_sh...  1.77 us

profile of v6, /device:TPU:0, one launch (start us, length us, event | category | flops | bytes accessed | tf_op | source)
XLA Modules:
  0.0 41.3 jit_solution(6163171170743427842)
XLA Ops:
  0.6 38.9 %step.1 = (f32[4,8,128]{2,1,0:T(8,128)}, f32[4,8,128]{2,1,0:T(8,128)}, bf16[8,56,128]{2,1,0:T(8,128)(2,1)}) custom-call(f32[4,8,128]{2,1,0:T(8,128)} %volume_hbm.1, bf16[4,8,128]{2,1,0:T(8,128)(2,1)} %upstream_hbm.1, f32[32,128]{1,0:T(8,128)} %bitcast.17, f32[32,128]{1,0:T(8,128)} %bitcast.18, s32[4,16,64]{2,1,0:T(8,128)} %bitcast.15, s32[4,64]{1,0:T(4,128)} %bitcast.20, ...), custom_call_target="tpu_custom_call" | custom-call | tf_op jit(solution)/shard_map/step/pallas_call | solution.py:874
  39.5 1.8 %emit.1 = (f32[4,8,128]{2,1,0:T(8,128)}, f32[4,8,128]{2,1,0:T(8,128)}, f32[9,6,32]{2,1,0:T(8,128)}, f32[1,32]{1,0:T(1,128)}, f32[9,32,96]{2,1,0:T(8,128)}, /*index=5*/f32[1,32]{1,0:T(1,128)}, f32[9,1,96]{2,1,0:T(1,128)}) custom-call(f32[4,8,128]{2,1,0:T(8,128)} %get-tuple-element.17.new_ref, f32[4,8,128]{2,1,0:T(8,128)} %get-tuple-element.18.grad_ref, ...), custom_call_target="tpu_custom_call" | custom-call | tf_op jit(solution)/shard_map/emit/pallas_call | solution.py:983
